TPU v7x, 32 devices: a whole 2x2x4 slice. The times are simulated.
32 devices in a mesh: rve: 2 (over x), sub: 16 (over z, y, core).
Axes of the slice: x: 2, y: 2, z: 4, core: 2. Of those that a mesh axis runs over, the one named last changes fastest.
Arguments:
- condensed: float32 [49152, 1536], P(('rve', 'sub')), parts along dimension 0, may hold values from -0.15625 to 0.15625
- eigen_loads: float32 [49152, 128], P(('rve', 'sub')), parts along dimension 0, may hold values from -6 to 6
- coarse_inverse: float32 [1536, 768], P(('rve', 'sub')), parts along dimension 0, may hold values from -0.21875 to 0.21875
- face_rows: int32 [16, 2, 128], P('sub'), may hold values from 0 to 1535, as said below
- primal_rows: int32 [16, 96], P('sub'), may hold values from 0 to 1535, as said below
- primal_slot: int32 [16, 96], P('sub'), may hold values from 0 to 95, each once within a row
Outputs:
- displaced: float32 [49152, 128], P(('rve', 'sub')), parts along dimension 0
- multipliers: float32 [4096, 128], P(('rve', 'sub')), parts along dimension 0
There are 2 independent parts, one for each index of `rve`. A program takes and returns all parts, laid end to end along the dimension named above; an argument that names none is the same for every part. Nothing has to cross between parts.
Inputs may be any that keep to these rules, and one draw needn't show every extreme that they name: `face_rows`: in each subdomain the 128 left-face rows, the 128 right-face rows and the 96 primal rows in primal_rows are all distinct. `primal_rows`: distinct from that subdomain's face rows.
All inputs are finite; a program needn't handle non-finite values.
Results may differ from a plain program's by a relative error of at most 0.0001.
Values sent between devices are 32-bit elements; how exact they have to be, the bound alone decides.
A program may use at most 64 MiB of HBM per device.

v0:
```python
import functools

import jax
import jax.numpy as jnp
from jax import lax
from jax.experimental import pallas as pl
from jax.experimental.pallas import tpu as pltpu
from jax.sharding import PartitionSpec as P

ITERS = 3
DAMPING = 0.5
VMEM_LIMIT = 67043328
MESH = pl.DeviceIdType.MESH
F32 = jnp.float32
BF16 = jnp.bfloat16
LANES = 128


def grid_of(count):
    chips = count // 2
    inner = 1
    while (2 * inner) ** 2 <= chips and chips % (2 * inner) == 0:
        inner *= 2
    return chips // inner, inner


def flipped(index, mask, count):
    if count & (count - 1):
        return lax.rem(index + count - mask, count)
    out = 0
    bit = 1
    while bit < count:
        own = lax.rem(index // bit, 2)
        out = out + bit * ((1 - own) if mask & bit else own)
        bit *= 2
    return out


def returned(index, mask, count):
    if count & (count - 1):
        return lax.rem(index + mask, count)
    return flipped(index, mask, count)


def split(value):
    high = value.astype(BF16)
    return high, (value - high.astype(F32)).astype(BF16)


def product(high, low, value):
    value_high, value_low = split(value)
    return product_parts(high, low, value_high, value_low)


def product_parts(high, low, value_high, value_low):
    width = value_high.shape[1]
    both = jnp.dot(high, jnp.concatenate([value_high, value_low], axis=1), preferred_element_type=F32)
    return both[:, :width] + both[:, width:] + jnp.dot(low, value_high, preferred_element_type=F32)


def kernel(
    count, primal, width, face_s, prim_s, face_hbm, prim_hbm, slot_hbm, k_hbm, f_hbm, cinv_hbm, pre_ref, kph_ref, kpl_ref, q_ref, lam_ref,
    face_v, prim_v, slot_v, f_ref, cinv_ref, in_sem, k_ref, kh_ref, kl_ref, e_ref, fh_ref, fl_ref, ks_ref, first_ref, ah_ref, al_ref, cols_ref, ch_ref, cl_ref,
    gat_ref, r_ref, send_r, send_l, got_r, got_l, send_ar, send_al, got_ar, got_al,
    k_sem, send_sem, block_sem, face_sem, cinv_send, cinv_recv, a_send, a_recv,
):
    outer, inner = grid_of(count)
    order, columns = f_ref.shape
    owned = primal // 2
    tile = order // k_sem.shape[0]
    padded = e_ref.shape[1]
    me = lax.axis_index("sub")
    core = lax.rem(me, 2)
    y = lax.rem(me // 2, inner)
    z = me // (2 * inner)

    def at(z_, y_, core_):
        return (z_ * inner + y_) * 2 + core_

    def around(steps):
        return lax.rem(me + (steps + count), count)

    def k_copy(c):
        rows = pl.ds(c * tile, tile)
        return pltpu.make_async_copy(k_hbm.at[rows, :], k_ref.at[rows, :], k_sem.at[c])

    held = [
        pltpu.make_async_copy(src, dst, in_sem.at[i])
        for i, (src, dst) in enumerate((
            (f_hbm, f_ref), (cinv_hbm, cinv_ref), (face_hbm, face_v), (prim_hbm, prim_v), (slot_hbm, slot_v)
        ))
    ]
    for copy in held:
        copy.start()
    for c in range(k_sem.shape[0]):
        k_copy(c).start()

    outer_peers = [at(flipped(z, m, outer), y, core) for m in range(1, outer)]
    outer_back = [returned(z, m, outer) for m in range(1, outer)]
    inner_peers = [at(z, flipped(y, m, inner), core) for m in range(1, inner)]
    partner = at(z, y, 1 - core)
    ring = [around(d) for d in (-1, 1)]

    barrier = pltpu.get_barrier_semaphore()
    greeted = outer_peers + inner_peers + [partner] + ring
    if outer & (outer - 1):
        greeted = greeted + [at(b, y, core) for b in outer_back]
    for peer in greeted:
        pl.semaphore_signal(barrier, inc=1, device_id={"sub": peer}, device_id_type=MESH)

    def remote(src, dst, ssem, rsem, peer):
        return pltpu.make_async_remote_copy(
            src_ref=src, dst_ref=dst, send_sem=ssem, recv_sem=rsem, device_id={"sub": peer}, device_id_type=MESH
        )

    cinv_copies = [
        remote(cinv_ref, cols_ref.at[slot], cinv_send.at[slot], cinv_recv.at[slot], around(d))
        for slot, d in ((0, 1), (1, -1))
    ]
    passed_on = remote(cols_ref.at[1], cols_ref.at[2], cinv_send.at[2], cinv_recv.at[2], around(-1))

    for copy in held:
        copy.wait()

    square = (primal, primal)
    eye = lax.broadcasted_iota(jnp.int32, square, 0) == lax.broadcasted_iota(jnp.int32, square, 1)
    prim_col = jnp.sum(jnp.where(eye, prim_v[...].astype(F32), 0.0), axis=1, keepdims=True)
    slot_col = jnp.sum(jnp.where(eye, slot_v[...].astype(F32), 0.0), axis=1, keepdims=True)
    corner_width = padded - 2 * width
    lane = lax.broadcasted_iota(jnp.int32, (primal, corner_width), 1).astype(F32)
    ordered = jnp.sum(jnp.where(slot_col == lane, prim_col + 1.0, 0.0), axis=0, keepdims=True) - 1.0
    ordering = jnp.where(lax.broadcasted_iota(jnp.int32, square, 0) == slot_v[...], 1.0, 0.0).astype(BF16)

    fh, fl = split(f_ref[...])
    fh_ref[...] = fh
    fl_ref[...] = fl

    def stream(first_tile, last_tile):
        @pl.loop(first_tile, last_tile)
        def _(c):
            k_copy(c).wait()
            rows = pl.ds(pl.multiple_of(c * tile, tile), tile)
            high, low = split(k_ref[rows, :])
            kh_ref[rows, :] = high
            kl_ref[rows, :] = low
            pre_ref[rows, :] = product_parts(high, low, fh_ref[...], fl_ref[...])

    half = 1
    stream(0, half)
    pl.semaphore_wait(barrier, len(greeted))
    for copy in cinv_copies:
        copy.start()
    stream(half, order // tile)

    used = 2 * width + primal

    def picked(to_ref, from_ref):
        def rows_of(start, size, row_at):
            @pl.loop(0, size // 8)
            def _(i):
                base = pl.multiple_of(i * 8, 8)
                for j in range(8):
                    to_ref[pl.ds(start + base + j, 1), :] = from_ref[pl.ds(row_at(base + j), 1), :]

        rows_of(0, width, lambda i: face_s[0, 1, i])
        rows_of(width, width, lambda i: face_s[0, 0, i])
        rows_of(2 * width, primal, lambda i: prim_s[0, i])

    def in_order(value):
        high, low = split(value)
        half_width = value.shape[1]
        both = jnp.dot(ordering, jnp.concatenate([high, low], axis=1), preferred_element_type=F32)
        return both[:, :half_width] + both[:, half_width:]

    picked(first_ref, pre_ref)
    empty = jnp.zeros((padded - used, columns), F32)
    first = jnp.concatenate([first_ref[:2 * width], in_order(first_ref[2 * width:used]), empty], axis=0)

    def one_hot_columns():
        right_ids, left_ids = face_v[0, 1:2, :], face_v[0, 0:1, :]
        ordered_ids = ordered.astype(jnp.int32)

        @pl.loop(0, order // tile)
        def _(c):
            rows = pl.ds(pl.multiple_of(c * tile, tile), tile)
            near = lax.broadcasted_iota(jnp.int32, (tile, width), 0) + c * tile
            e_ref[rows, :width] = jnp.where(near == right_ids, 1.0, 0.0).astype(BF16)
            e_ref[rows, width:2 * width] = jnp.where(near == left_ids, 1.0, 0.0).astype(BF16)
            near = lax.broadcasted_iota(jnp.int32, (tile, corner_width), 0) + c * tile
            e_ref[rows, 2 * width:] = jnp.where(near == ordered_ids, 1.0, 0.0).astype(BF16)

    def finish_a():
        one_hot_columns()
        if padded > used:
            ks_ref[used:, :] = jnp.zeros((padded - used, order), F32)
        picked(ks_ref, k_ref)
        high, low = split(ks_ref[...])
        parts = []
        for part, out in ((high, ah_ref), (low, al_ref)):
            found = jnp.dot(part, e_ref[...], preferred_element_type=F32)
            out[:2 * width, :] = found[:2 * width].astype(BF16)
            out[2 * width:used, :] = jnp.dot(
                ordering, found[2 * width:used].astype(BF16), preferred_element_type=F32
            ).astype(BF16)
            if padded > used:
                out[used:, :] = jnp.zeros((padded - used, padded), BF16)
            parts.append(found[:2 * width, 2 * width:])
        corner = parts[0] + parts[1]
        send_ar[...] = corner[:width]
        send_al[...] = corner[width:]

    def primal_columns():
        picks = e_ref[:, 2 * width:]

        @pl.loop(0, order // tile)
        def _(c):
            rows = pl.ds(pl.multiple_of(c * tile, tile), tile)
            kph_ref[rows, :] = jnp.dot(kh_ref[rows, :], picks, preferred_element_type=F32).astype(BF16)
            kpl_ref[rows, :] = jnp.dot(kl_ref[rows, :], picks, preferred_element_type=F32).astype(BF16)

    def uncorrected(changes):
        high, low = split(changes)
        spread = jnp.dot(e_ref[:, :2 * width], jnp.concatenate([high, low], axis=1), preferred_element_type=F32)
        loads = f_ref[...] + (spread[:, :columns] + spread[:, columns:])
        high, low = split(loads)
        fh_ref[...] = high
        fl_ref[...] = low

        @pl.loop(0, order // tile)
        def _(c):
            rows = pl.ds(pl.multiple_of(c * tile, tile), tile)
            pre_ref[rows, :] = product_parts(kh_ref[rows, :], kl_ref[rows, :], fh_ref[...], fl_ref[...])

    a_copies = [
        remote(send_al, got_al, a_send.at[0], a_recv.at[0], around(-1)),
        remote(send_ar, got_ar, a_send.at[1], a_recv.at[1], around(1)),
    ]

    lam = jnp.zeros((width, columns), F32)
    lam_before = jnp.zeros((width, columns), F32)
    values = first
    changes = None
    for step in range(ITERS):
        if step:
            changes = jnp.concatenate([-lam, lam_before], axis=0)
            values = first + product(ah_ref[:, :2 * width], al_ref[:, :2 * width], changes)
        gat = gat_ref.at[step]
        gat_ref[step, me] = values[2 * width:2 * width + primal]
        send_r[step] = values[:width]
        send_l[step] = values[width:2 * width]
        started = []

        def forward(block, peer, part):
            rows = gat.at[block, pl.ds(part * owned, owned)]
            copy = remote(rows, rows, send_sem.at[step, len(started)], block_sem.at[step, block, part], peer)
            copy.start()
            started.append(copy)

        def arrived(block, part):
            rows = gat.at[block, pl.ds(part * owned, owned)]
            remote(rows, rows, send_sem.at[step, 0], block_sem.at[step, block, part], partner).wait_recv()

        for part in range(2):
            for peer in reversed(outer_peers):
                forward(me, peer, part)
            for peer in inner_peers:
                forward(me, peer, part)
            forward(me, partner, part)
        faces = [
            remote(send_l.at[step], got_l.at[step], face_sem.at[0, step, 0], face_sem.at[1, step, 0], around(-1)),
            remote(send_r.at[step], got_r.at[step], face_sem.at[0, step, 1], face_sem.at[1, step, 1], around(1)),
        ]
        for copy in faces:
            copy.start()

        if step == 0:
            cinv_copies[1].wait_recv()
            passed_on.start()
            finish_a()
            for copy in a_copies:
                copy.start()
        if step == 1:
            primal_columns()
        if step == ITERS - 1:
            uncorrected(changes)

        for part in range(2):
            for source in outer_back:
                block = at(source, y, core)
                arrived(block, part)
                for peer in inner_peers:
                    forward(block, peer, part)
                forward(block, partner, part)
        if step == 0:
            cinv_copies[0].wait()
            cinv_copies[1].wait_send()
            passed_on.wait()
            for slot, part in enumerate((cols_ref.at[0], cinv_ref, cols_ref.at[1], cols_ref.at[2])):
                high, low = split(part[...])
                ch_ref[slot * owned:(slot + 1) * owned, :] = high
                cl_ref[slot * owned:(slot + 1) * owned, :] = low
        for part in range(2):
            for m in range(1, inner):
                for source in [z] + outer_back:
                    block = at(source, returned(y, m, inner), core)
                    arrived(block, part)
                    forward(block, partner, part)
        for part in range(2):
            for source in [z] + outer_back:
                for m in range(inner):
                    arrived(at(source, y if m == 0 else returned(y, m, inner), 1 - core), part)

        for s in range(count):
            r_ref[s * owned:(s + 1) * owned, :] = (
                gat_ref[step, s, :owned, :] + gat_ref[step, (s - 1) % count, owned:, :]
            )
        coarse = product(ch_ref[...], cl_ref[...], r_ref[...])
        fill = jnp.zeros((padded - 2 * width - primal, columns), F32)

        def steps_of(slot):
            return jnp.concatenate([coarse[slot * owned:(slot + 2) * owned], fill], axis=0)

        q_before, q_own, q_after = steps_of(0), steps_of(1), steps_of(2)
        own = product(ah_ref[:2 * width, 2 * width:], al_ref[:2 * width, 2 * width:], q_own)
        if step == 0:
            for copy in a_copies:
                copy.wait()
        for copy in faces:
            copy.wait()
        after = product(*split(got_al[...]), q_after)
        lam = lam + DAMPING * ((values[:width] - own[:width]) - (got_l[step] - after))
        if step + 1 < ITERS:
            before = product(*split(got_ar[...]), q_before)
            lam_before = lam_before + DAMPING * ((got_r[step] - before) - (values[width:2 * width] - own[width:]))
        else:
            lam_ref[...] = lam
            q_ref[...] = q_own
        for copy in started:
            copy.wait_send()


def finish(pre_ref, kph_ref, kpl_ref, q_ref, lam_ref, u_ref, lam_out):
    u_ref[...] = pre_ref[...] - product(kph_ref[...], kpl_ref[...], q_ref[...])
    lam_out[...] = lam_ref[...]


def local(condensed, eigen_loads, coarse_inverse, face_rows, primal_rows, primal_slot):
    count = lax.axis_size("sub")
    order, columns = eigen_loads.shape
    owned, total = coarse_inverse.shape
    width = face_rows.shape[2]
    primal = primal_rows.shape[1]
    padded = 2 * width + -(-primal // LANES) * LANES
    outer, inner = grid_of(count)
    corner_width = padded - 2 * width
    tile = 256 if order % 256 == 0 else order
    sends = (outer - 1) + (inner - 1) * outer + outer * inner
    dma = pltpu.SemaphoreType.DMA
    vmem = pl.BlockSpec(memory_space=pltpu.VMEM)
    face = pltpu.VMEM((ITERS, width, columns), F32)
    corner = pltpu.VMEM((width, padded - 2 * width), F32)
    smem = pl.BlockSpec(memory_space=pltpu.SMEM)
    needed = 8 * order * (order + padded + 2 * columns) + 4 * padded * (order + columns + padded)
    needed += 4 * owned * total * 8 + 4 * columns * (ITERS * (count * primal + 4 * width) + total)
    needed += 4 * order * (columns + 2 * corner_width) + 4 * columns * (order + 8 * width)
    shape = jax.ShapeDtypeStruct
    held = [
        pltpu.with_memory_space_constraint(value, pltpu.HBM)
        for value in (face_rows, primal_rows, primal_slot, condensed, eigen_loads, coarse_inverse)
    ]
    parts = pl.pallas_call(
        functools.partial(kernel, count, primal, width),
        out_shape=(
            shape((order, columns), F32),
            shape((order, corner_width), BF16),
            shape((order, corner_width), BF16),
            shape((corner_width, columns), F32),
            shape((width, columns), F32),
        ),
        in_specs=[smem, smem] + [pl.BlockSpec(memory_space=pltpu.HBM)] * 6,
        out_specs=(vmem,) * 5,
        scratch_shapes=[
            pltpu.VMEM(face_rows.shape, jnp.int32),
            pltpu.VMEM(primal_rows.shape, jnp.int32),
            pltpu.VMEM(primal_slot.shape, jnp.int32),
            pltpu.VMEM((order, columns), F32),
            pltpu.VMEM((owned, total), F32),
            dma((5,)),
            pltpu.VMEM((order, order), F32),
            pltpu.VMEM((order, order), BF16),
            pltpu.VMEM((order, order), BF16),
            pltpu.VMEM((order, padded), BF16),
            pltpu.VMEM((order, columns), BF16),
            pltpu.VMEM((order, columns), BF16),
            pltpu.VMEM((padded, order), F32),
            pltpu.VMEM((padded, columns), F32),
            pltpu.VMEM((padded, padded), BF16),
            pltpu.VMEM((padded, padded), BF16),
            pltpu.VMEM((3, owned, total), F32),
            pltpu.VMEM((4 * owned, total), BF16),
            pltpu.VMEM((4 * owned, total), BF16),
            pltpu.VMEM((ITERS, count, primal, columns), F32),
            pltpu.VMEM((total, columns), F32),
            face, face, face, face,
            corner, corner, corner, corner,
            dma((order // tile,)),
            dma((ITERS, 2 * sends)),
            dma((ITERS, count, 2)),
            dma((2, ITERS, 2)),
            dma((3,)),
            dma((3,)),
            dma((2,)),
            dma((2,)),
        ],
        compiler_params=pltpu.CompilerParams(
            collective_id=0, has_side_effects=True, vmem_limit_bytes=min(VMEM_LIMIT, needed + needed // 4)
        ),
    )(face_rows, primal_rows, *held)
    return pl.pallas_call(
        finish,
        out_shape=(shape((order, columns), F32), shape((width, columns), F32)),
        in_specs=[vmem] * 5,
        out_specs=(vmem, vmem),
        compiler_params=pltpu.CompilerParams(vmem_limit_bytes=4 * order * columns * 8),
    )(*parts)


def solution(mesh):
    placed = (
        P(("rve", "sub"), None),
        P(("rve", "sub"), None),
        P(("rve", "sub"), None),
        P("sub", None, None),
        P("sub", None),
        P("sub", None),
    )
    return jax.shard_map(
        local,
        mesh=mesh,
        in_specs=placed,
        out_specs=(P(("rve", "sub"), None), P(("rve", "sub"), None)),
        check_vma=False,
    )
```

profile of v0, /device:TPU:0, one launch (start us, length us, event | category | flops | bytes accessed | tf_op | source)
XLA Modules:
  0.0 51.0 jit_solution(9938959438042218805)
XLA Ops:
  0.6 49.0 %shard_map.77 = (f32[1536,128]{1,0:T(8,128)S(1)}, bf16[1536,128]{1,0:T(8,128)(2,1)S(1)}, bf16[1536,128]{1,0:T(8,128)(2,1)S(1)}, f32[128,128]{1,0:T(8,128)S(1)}, f32[128,128]{1,0:T(8,128)S(1)}) custom-call(s32[1,2,128]{2,1,0:T(2,128)} %face_hbm.1, s32[1,96]{1,0:T(1,128)} %prim_hbm.1, s32[1,2,128]{2,1,0:T(2,128)} %face_hbm.1, s32[1,96]{1,0:T(1,128)} %prim_hbm.1, ...), custom_call_target="tpu_custom_call" | custom-call | tf_op jit(solution)/shard_map/pallas_call | solution.py:371
  49.7 1.3 %shard_map.78 = (f32[1536,128]{1,0:T(8,128)}, f32[128,128]{1,0:T(8,128)}) custom-call(f32[1536,128]{1,0:T(8,128)S(1)} %get-tuple-element.7.pre_ref, bf16[1536,128]{1,0:T(8,128)(2,1)S(1)} %get-tuple-element.8.kph_ref, bf16[1536,128]{1,0:T(8,128)(2,1)S(1)} %get-tuple-element.9.kpl_ref, f32[128,128]{1,0:T(8,128)S(1)} %get-tuple-element.10.q_ref, ...), custom_call_target="tpu_custom_call" | custom-call | tf_op jit(solution)/shard_map/pallas_call | solution.py:419
where the time goes:
time: 51.8 us; the launch traced here: 51 us
  Pallas kernels  50.4 us (97%)
  between operations  0.64 us (1%)
    pallas_call x1, Pallas kernels, local(): pl.pallas_call(functools.partial(kernel, count, primal, width), out_shape...  49 us
    pallas_call x1, Pallas kernels, local(): pl.pallas_call(finish, out_shape=(shape((order, columns), F32), shape((wi...  1.35 us

commit v1 on v0

--- a/solution.py
+++ b/solution.py
@@ -14,6 +14,7 @@
 F32 = jnp.float32
 BF16 = jnp.bfloat16
 LANES = 128
+PLANE_LIMIT = 60 * 1024 * 1024
 
 
 def grid_of(count):
@@ -344,7 +345,608 @@
     lam_out[...] = lam_ref[...]
 
 
-def local(condensed, eigen_loads, coarse_inverse, face_rows, primal_rows, primal_slot):
+NT = (((1,), (1,)), ((), ()))
+NN = (((1,), (0,)), ((), ()))
+
+
+def tall(x, high, low, dims):
+    x_high, x_low = split(x)
+    count = x.shape[0]
+    both = lax.dot_general(jnp.concatenate([x_high, x_low], axis=0), high, dims, preferred_element_type=F32)
+    return both[:count] + both[count:] + lax.dot_general(x_high, low, dims, preferred_element_type=F32)
+
+
+def lanes_of(count):
+    return -(-count // LANES) * LANES
+
+
+def plane_kernel(
+    count, primal, width, face_hbm, prim_hbm, slot_hbm, k_hbm, f_hbm, cinv_hbm, pre_ref, kph_ref, kpl_ref, q_ref, lam_ref,
+    face_s, prim_s, face_v, prim_v, slot_v, f_ref, k_ref, kh_ref, kl_ref, e_ref, fh_ref, fl_ref, ks_ref,
+    own_c, own_b, c_in, b_in, cinv_ref, cqh_ref, cql_ref, ac_ref, ap_ref, ar_ref, before_ref, after_ref,
+    ach_ref, acl_ref, aph_ref, apl_ref, arh_ref, arl_ref, r_ref, face_out, face_in, x_out, x_in, q_out, q_in, lam_out, lam_in,
+    in_sem, k_sem, c_sem, b_sem, cinv_send, cinv_recv, ac_send, ac_recv, ap_send, ap_recv, ar_send, ar_recv,
+    halo_send, halo_recv, edge_sem, r_sem, face_sem, x_sem, q_sem, lam_sem,
+):
+    outer, inner = grid_of(count)
+    plane = 2 * inner
+    order, columns = f_ref.shape
+    owned = primal // 2
+    total = cinv_ref.shape[-1]
+    tiles = k_sem.shape[0]
+    tile = order // tiles
+    share = columns // plane
+    both = 2 * width
+    wide = lanes_of(primal)
+    span = r_ref.shape[-1]
+    me = lax.axis_index("sub")
+    mine = lax.rem(me, plane)
+    z = me // plane
+    core = lax.rem(me, 2)
+
+    def at(z_, mine_):
+        return z_ * plane + mine_
+
+    partner = at(z, mine + 1 - 2 * core)
+    across = [lax.rem(mine + 2 * m, plane) for m in range(1, inner)]
+    across_peers = [at(z, other) for other in across]
+    others = [lax.rem(mine + m, plane) for m in range(1, plane)]
+    mates = [at(z, other) for other in others]
+    beyond = [at(lax.rem(z + m, outer), mine) for m in range(1, outer)]
+    after, before = beyond[0], beyond[-1]
+
+    def remote(src, dst, ssem, rsem, peer):
+        return pltpu.make_async_remote_copy(
+            src_ref=src, dst_ref=dst, send_sem=ssem, recv_sem=rsem, device_id={"sub": peer}, device_id_type=MESH
+        )
+
+    def send(src, dst, ssem, rsem, peer):
+        remote(src, dst, ssem, rsem, peer).start()
+
+    def arrived(ref, rsem):
+        remote(ref, ref, r_sem.at[0, 0], rsem, partner).wait_recv()
+
+    def sent(ref, ssem):
+        remote(ref, ref, ssem, r_sem.at[0, 1], partner).wait_send()
+
+    ints = [
+        pltpu.make_async_copy(src, dst, in_sem.at[i])
+        for i, (src, dst) in enumerate((
+            (face_hbm, face_s), (prim_hbm, prim_s), (face_hbm, face_v), (prim_hbm, prim_v), (slot_hbm, slot_v)
+        ))
+    ]
+    cinv_copy = pltpu.make_async_copy(cinv_hbm, cinv_ref.at[mine + 1], in_sem.at[5])
+    f_copy = pltpu.make_async_copy(f_hbm, f_ref, in_sem.at[6])
+
+    def k_copy(c):
+        rows = pl.ds(c * tile, tile)
+        return pltpu.make_async_copy(k_hbm.at[rows, :], k_ref.at[rows, :], k_sem.at[c])
+
+    for copy in ints + [cinv_copy, f_copy]:
+        copy.start()
+    for c in range(tiles):
+        k_copy(c).start()
+
+    barrier = pltpu.get_barrier_semaphore()
+    for peer in mates + beyond:
+        pl.semaphore_signal(barrier, inc=1, device_id={"sub": peer}, device_id_type=MESH)
+
+    with jax.named_scope("P_ints"):
+        for copy in ints:
+            copy.wait()
+    square = (primal, primal)
+    eye = lax.broadcasted_iota(jnp.int32, square, 0) == lax.broadcasted_iota(jnp.int32, square, 1)
+    prim_col = jnp.sum(jnp.where(eye, prim_v[...].astype(F32), 0.0), axis=1, keepdims=True)
+    slot_col = jnp.sum(jnp.where(eye, slot_v[...].astype(F32), 0.0), axis=1, keepdims=True)
+    lane = lax.broadcasted_iota(jnp.int32, (primal, wide), 1).astype(F32)
+    ordered = jnp.sum(jnp.where(slot_col == lane, prim_col + 1.0, 0.0), axis=0, keepdims=True) - 1.0
+    ordering = jnp.where(lax.broadcasted_iota(jnp.int32, (wide, primal), 0) == slot_v[...], 1.0, 0.0).astype(BF16)
+
+    def in_order(value):
+        high, low = split(value)
+        size = value.shape[1]
+        pair = jnp.dot(ordering, jnp.concatenate([high, low], axis=1), preferred_element_type=F32)
+        return pair[:, :size] + pair[:, size:]
+
+    def one_hot_columns():
+        right_ids, left_ids = face_v[0, 1:2, :], face_v[0, 0:1, :]
+        ordered_ids = ordered.astype(jnp.int32)
+
+        @pl.loop(0, tiles)
+        def _(c):
+            rows = pl.ds(pl.multiple_of(c * tile, tile), tile)
+            near = lax.broadcasted_iota(jnp.int32, (tile, width), 0) + c * tile
+            e_ref[rows, :width] = jnp.where(near == right_ids, 1.0, 0.0).astype(BF16)
+            e_ref[rows, width:both] = jnp.where(near == left_ids, 1.0, 0.0).astype(BF16)
+            near = lax.broadcasted_iota(jnp.int32, (tile, wide), 0) + c * tile
+            e_ref[rows, both:] = jnp.where(near == ordered_ids, 1.0, 0.0).astype(BF16)
+
+    def spread(buf, ssem, rsem, own):
+        for peer in across_peers + [partner]:
+            send(buf.at[own], buf.at[own], ssem, rsem.at[own], peer)
+
+    def relay(buf, ssem, rsem, shift=0):
+        for other in across:
+            block = other + shift
+            arrived(buf.at[block], rsem.at[block])
+            send(buf.at[block], buf.at[block], ssem, rsem.at[block], partner)
+
+    def settle(buf, rsem, shift=0):
+        for other in [mine] + across:
+            block = other + 1 - 2 * core + shift
+            arrived(buf.at[block], rsem.at[block])
+
+    with jax.named_scope("P_onehot"):
+        one_hot_columns()
+    with jax.named_scope("P_barrier"):
+        pl.semaphore_wait(barrier, len(mates + beyond))
+        cinv_copy.wait()
+    spread(cinv_ref, cinv_send, cinv_recv, mine + 1)
+
+    with jax.named_scope("P_f"):
+        f_copy.wait()
+        high, low = split(f_ref[...])
+        fh_ref[...] = high
+        fl_ref[...] = low
+
+    def halve(first_tile, last_tile):
+        @pl.loop(first_tile, last_tile)
+        def _(c):
+            rows = pl.ds(pl.multiple_of(c * tile, tile), tile)
+            high, low = split(k_ref[rows, :])
+            kh_ref[rows, :] = high
+            kl_ref[rows, :] = low
+
+    with jax.named_scope("P_kwait"):
+        for c in range(tiles):
+            k_copy(c).wait()
+
+    def picked(start, size, row_at):
+        @pl.loop(0, size // 8)
+        def _(i):
+            base = pl.multiple_of(i * 8, 8)
+            for j in range(8):
+                ks_ref[pl.ds(start + base + j, 1), :] = k_ref[pl.ds(row_at(base + j), 1), :]
+
+    def first(rows):
+        high, low = split(ks_ref[rows, :])
+        return product_parts(high, low, fh_ref[...], fl_ref[...])
+
+    with jax.named_scope("P_first"):
+        picked(both, primal, lambda i: prim_s[0, i])
+        own_c[...] = in_order(first(slice(both, both + primal))).T.reshape(own_c.shape)
+        for other, peer in zip(others, mates):
+            send(own_c.at[other], c_in.at[mine], c_sem.at[0], c_sem.at[1], peer)
+        c_in[mine] = own_c[mine]
+    with jax.named_scope("P_firstb"):
+        picked(0, width, lambda i: face_s[0, 1, i])
+        picked(width, width, lambda i: face_s[0, 0, i])
+        loads = first(slice(0, both))
+        own_b[:, :, :width] = loads[:width].T.reshape(plane, share, width)
+        own_b[:, :, width:] = loads[width:].T.reshape(plane, share, width)
+        for other, peer in zip(others, mates):
+            send(own_b.at[other], b_in.at[mine], b_sem.at[0], b_sem.at[1], peer)
+        b_in[mine] = own_b[mine]
+    def assembled(parts):
+        sums = None
+        for i, part in enumerate(parts):
+            part = jnp.concatenate([part, jnp.zeros((share, span - wide), F32)], axis=1)
+            part = pltpu.roll(part, owned * i, 1) if i else part
+            sums = part if sums is None else sums + part
+        return sums
+
+    def publish(step, parts):
+        r_ref[step, z] = assembled(parts)
+        for peer in reversed(beyond):
+            rows = r_ref.at[step, z]
+            send(rows, rows, r_sem.at[step, 0], r_sem.at[step, 1], peer)
+
+    def faces(step, last_right, first_left):
+        face_out[step, 0] = first_left
+        send(face_out.at[step, 0], face_in.at[step, 0], face_sem.at[step, 0], face_sem.at[step, 1], before)
+        if step + 1 < ITERS:
+            face_out[step, 1] = last_right
+            send(face_out.at[step, 1], face_in.at[step, 1], face_sem.at[step, 0], face_sem.at[step, 1], after)
+
+    def face_part(ref, step):
+        return ref.at[step] if step + 1 < ITERS else ref.at[step, pl.ds(0, 1)]
+
+    def columns_of(rows, picks):
+        high, low = split(ks_ref[rows, :])
+        return jnp.dot(high, picks, preferred_element_type=F32) + jnp.dot(low, picks, preferred_element_type=F32)
+
+    def primal_columns(first_tile, last_tile):
+        picks = e_ref[:, both:]
+
+        @pl.loop(first_tile, last_tile)
+        def _(c):
+            rows = pl.ds(pl.multiple_of(c * tile, tile), tile)
+            kph_ref[rows, :] = jnp.dot(kh_ref[rows, :], picks, preferred_element_type=F32).astype(BF16)
+            kpl_ref[rows, :] = jnp.dot(kl_ref[rows, :], picks, preferred_element_type=F32).astype(BF16)
+
+    def coarse_rows(blocks):
+        for b in blocks:
+            high, low = split(cinv_ref[b])
+            for pair, half in ((b, 0), (b - 1, 1)):
+                if 0 <= pair < plane + 2:
+                    start = pair * wide + half * owned
+                    cqh_ref[start:start + owned, :] = high
+                    cql_ref[start:start + owned, :] = low
+
+    def halves_of(refs, src):
+        for i in range(plane):
+            for ref, part in zip(refs, split(src[i])):
+                ref[i, :primal, :] = part
+                ref[i, primal:, :] = jnp.zeros((wide - primal, both), BF16)
+
+    with jax.named_scope("P_ac"):
+        found = columns_of(slice(0, both), e_ref[:, both:])
+        ac_ref[mine, :, :width] = found[:width].T[:primal]
+        ac_ref[mine, :, width:] = found[width:].T[:primal]
+        spread(ac_ref, ac_send, ac_recv, mine)
+    with jax.named_scope("P_relayc"):
+        relay(cinv_ref, cinv_send, cinv_recv, 1)
+    with jax.named_scope("P_cwait"):
+        arrived(c_in.at[pl.ds(0, plane - 1)], c_sem.at[1])
+    publish(0, [c_in[i] for i in range(plane)])
+    with jax.named_scope("P_ap"):
+        ap_ref[mine] = in_order(columns_of(slice(both, both + primal), e_ref[:, :both]))[:primal]
+        spread(ap_ref, ap_send, ap_recv, mine)
+    with jax.named_scope("P_halo"):
+        settle(cinv_ref, cinv_recv, 1)
+        halves = owned // 2
+        near = cinv_ref.at[0, pl.ds(core * halves, halves)]
+        far = cinv_ref.at[plane + 1 + core]
+        send(cinv_ref.at[1 + core], far, halo_send.at[0], halo_recv.at[0], before)
+        send(cinv_ref.at[plane, pl.ds(core * halves, halves)], near, halo_send.at[1], halo_recv.at[1], after)
+    with jax.named_scope("P_bwait"):
+        arrived(b_in.at[pl.ds(0, plane - 1)], b_sem.at[1])
+    faces(0, b_in[plane - 1, :, :width], b_in[0, :, width:])
+
+    urgent = jnp.where(mine == 0, 1, 0)
+
+    def spread_half(half):
+        for peer in across_peers + [partner]:
+            rows = ar_ref.at[mine, half]
+            send(rows, rows, ar_send, ar_recv.at[mine, half], peer)
+
+    def relay_half(flip):
+        for other in across:
+            half = jnp.where(other == 0, 1 - flip, flip)
+            rows = ar_ref.at[other, half]
+            arrived(rows, ar_recv.at[other, half])
+            send(rows, rows, ar_send, ar_recv.at[other, half], partner)
+
+    def settle_half(flip):
+        for other in [mine] + across:
+            block = other + 1 - 2 * core
+            half = jnp.where(block == 0, 1 - flip, flip)
+            arrived(ar_ref.at[block, half], ar_recv.at[block, half])
+
+    with jax.named_scope("P_ar"):
+        found = columns_of(slice(0, both), e_ref[:, :both])
+        ar_ref[mine, 0] = found[:width]
+        ar_ref[mine, 1] = found[width:]
+    with jax.named_scope("P_halve"):
+        halve(0, tiles)
+    with jax.named_scope("P_cq"):
+        for ref in (cqh_ref, cql_ref):
+            for pair in range(plane + 2):
+                ref[pair * wide + primal:(pair + 1) * wide, :] = jnp.zeros((wide - primal, total), BF16)
+        coarse_rows(range(1, plane + 1))
+    with jax.named_scope("P_relayac"):
+        relay(ac_ref, ac_send, ac_recv)
+        spread_half(urgent)
+    with jax.named_scope("P_settleac"):
+        settle(ac_ref, ac_recv)
+        send(ac_ref.at[plane - 1, :, pl.ds(0, width)], before_ref, edge_sem.at[0], edge_sem.at[1], after)
+        send(ac_ref.at[0, :, pl.ds(width, width)], after_ref, edge_sem.at[0], edge_sem.at[2], before)
+        halves_of((ach_ref, acl_ref), ac_ref)
+    with jax.named_scope("P_halo2"):
+        arrived(far, halo_recv.at[0])
+        send(far, far, halo_send.at[0], halo_recv.at[2], partner)
+        arrived(near, halo_recv.at[1])
+        send(near, near, halo_send.at[1], halo_recv.at[3], partner)
+    with jax.named_scope("P_relayap"):
+        relay(ap_ref, ap_send, ap_recv)
+        spread_half(1 - urgent)
+    half_tiles = tiles // 2
+    with jax.named_scope("P_halo3"):
+        other_near = cinv_ref.at[0, pl.ds((1 - core) * halves, halves)]
+        other_far = cinv_ref.at[plane + 2 - core]
+        arrived(other_far, halo_recv.at[2])
+        arrived(other_near, halo_recv.at[3])
+        coarse_rows([0, plane + 1, plane + 2])
+
+    def uncorrected(first_tile, last_tile):
+        @pl.loop(first_tile, last_tile)
+        def _(c):
+            rows = pl.ds(pl.multiple_of(c * tile, tile), tile)
+            pre_ref[rows, :] = product_parts(kh_ref[rows, :], kl_ref[rows, :], fh_ref[...], fl_ref[...])
+
+    def changed_loads():
+        high, low = split(x_in[...].reshape(columns, both))
+        moved = lax.dot_general(
+            e_ref[:, :both], jnp.concatenate([high, low], axis=0), NT, preferred_element_type=F32
+        )
+        high, low = split(f_ref[...] + (moved[:, :columns] + moved[:, columns:]))
+        fh_ref[...] = high
+        fl_ref[...] = low
+
+    def padded(value):
+        return jnp.concatenate([value, jnp.zeros((wide - primal, value.shape[1]), F32)], axis=0)
+
+    lam = [jnp.zeros((share, width), F32)] * (plane + 1)
+    values = [b_in[i] for i in range(plane)]
+    edges = None
+    for step in range(ITERS):
+        if step == ITERS - 1:
+            with jax.named_scope("P_xwait"):
+                arrived(x_in.at[pl.ds(0, plane - 1)], x_sem.at[1])
+                changed_loads()
+            with jax.named_scope("P_uncorr0"):
+                uncorrected(0, half_tiles)
+        with jax.named_scope(f"P_rwait{step}"):
+            arrived(r_ref.at[step, pl.ds(0, outer - 1)], r_sem.at[step, 1])
+        with jax.named_scope(f"P_coarse{step}"):
+            sums = None
+            for i in range(outer):
+                part = jnp.concatenate([r_ref[step, i], jnp.zeros((share, total - span), F32)], axis=1)
+                part = pltpu.roll(part, plane * owned * i, 1) if i else part
+                sums = part if sums is None else sums + part
+            coarse = tall(sums, cqh_ref[...], cql_ref[...], NT)
+            steps = [coarse[:, i * wide:(i + 1) * wide] for i in range(plane + 2)]
+            if step == ITERS - 1:
+                for i in range(plane):
+                    q_out[i] = steps[i + 1]
+                for other, peer in zip(others, mates):
+                    send(q_out.at[other], q_in.at[mine], q_sem.at[0], q_sem.at[1], peer)
+                q_in[mine] = q_out[mine]
+        if edges is None:
+            with jax.named_scope("P_edge"):
+                arrived(before_ref, edge_sem.at[1])
+                arrived(after_ref, edge_sem.at[2])
+                edges = [split(padded(ref[...])) for ref in (before_ref, after_ref)]
+        with jax.named_scope(f"P_faces{step}"):
+            arrived(face_part(face_in, step), face_sem.at[step, 1])
+        with jax.named_scope(f"P_update{step}"):
+            moved = [values[i] - tall(steps[i + 1], ach_ref[i], acl_ref[i], NN) for i in range(plane)]
+            right = [part[:, :width] for part in moved]
+            left = [part[:, width:] for part in moved]
+            left.append(face_in[step, 0] - tall(steps[plane + 1], *edges[1], NN))
+            lam_next = [lam[i + 1] + DAMPING * (right[i] - left[i + 1]) for i in range(plane)]
+            if step + 1 < ITERS:
+                ahead = face_in[step, 1] - tall(steps[0], *edges[0], NN)
+                lam_next = [lam[0] + DAMPING * (ahead - left[0])] + lam_next
+            else:
+                for i in range(plane):
+                    lam_out[i] = lam_next[i]
+                for other, peer in zip(others, mates):
+                    send(lam_out.at[other], lam_in.at[mine], lam_sem.at[0], lam_sem.at[1], peer)
+                lam_in[mine] = lam_out[mine]
+                break
+            lam = lam_next
+            if step == 0:
+                with jax.named_scope("P_settleap"):
+                    settle(ap_ref, ap_recv)
+                    halves_of((aph_ref, apl_ref), ap_ref)
+            changes = [jnp.concatenate([-lam[i + 1], lam[i]], axis=1) for i in range(plane)]
+            publish(step + 1, [
+                c_in[i] + tall(changes[i], aph_ref[i], apl_ref[i], NT) for i in range(plane)
+            ])
+            if step == ITERS - 2:
+                for i in range(plane):
+                    x_out[i] = changes[i]
+                for other, peer in zip(others, mates):
+                    send(x_out.at[other], x_in.at[mine], x_sem.at[0], x_sem.at[1], peer)
+                x_in[mine] = x_out[mine]
+        if step == 0:
+            with jax.named_scope("P_relayr0"):
+                relay_half(0)
+                settle_half(0)
+                for i, half in ((plane - 1, 0), (0, 1)):
+                    rows = slice(half * width, (half + 1) * width)
+                    for ref, part in zip((arh_ref, arl_ref), split(ar_ref[i, half])):
+                        ref[i, rows] = part
+            with jax.named_scope("P_facevalues"):
+                last_right = tall(changes[-1], arh_ref[plane - 1, :width], arl_ref[plane - 1, :width], NT)
+                first_left = tall(changes[0], arh_ref[0, width:], arl_ref[0, width:], NT)
+                faces(1, b_in[plane - 1, :, :width] + last_right, b_in[0, :, width:] + first_left)
+            with jax.named_scope("P_primcol"):
+                primal_columns(0, half_tiles)
+            with jax.named_scope("P_relayr1"):
+                relay_half(1)
+            with jax.named_scope("P_primcol"):
+                primal_columns(half_tiles, tiles)
+            with jax.named_scope("P_settler1"):
+                settle_half(1)
+                for i in range(plane):
+                    for half in range(2):
+                        if (i, half) not in ((plane - 1, 0), (0, 1)):
+                            rows = slice(half * width, (half + 1) * width)
+                            for ref, part in zip((arh_ref, arl_ref), split(ar_ref[i, half])):
+                                ref[i, rows] = part
+        with jax.named_scope(f"P_values{step}"):
+            values = [b_in[i] + tall(changes[i], arh_ref[i], arl_ref[i], NT) for i in range(plane)]
+            if step:
+                faces(step + 1, values[plane - 1][:, :width], values[0][:, width:])
+
+    with jax.named_scope("P_uncorr1"):
+        uncorrected(half_tiles, tiles)
+    with jax.named_scope("P_qwait"):
+        arrived(q_in.at[pl.ds(0, plane - 1)], q_sem.at[1])
+        q_ref[...] = q_in[...].reshape(q_ref.shape)
+    with jax.named_scope("P_lamwait"):
+        arrived(lam_in.at[pl.ds(0, plane - 1)], lam_sem.at[1])
+        lam_ref[...] = lam_in[...].reshape(lam_ref.shape)
+    with jax.named_scope("P_sent"):
+        others_part = pl.ds(0, plane - 1)
+        sent(own_c.at[others_part], c_sem.at[0])
+        sent(own_b.at[others_part], b_sem.at[0])
+        sent(cinv_ref.at[others_part], cinv_send)
+        for ref, sem in ((ac_ref, ac_send), (ap_ref, ap_send), (ar_ref, ar_send)):
+            sent(ref.at[others_part], sem)
+        sent(cinv_ref.at[pl.ds(0, 2)], halo_send.at[0])
+        sent(cinv_ref.at[0], halo_send.at[1])
+        sent(ac_ref.at[0], edge_sem.at[0])
+        for step in range(ITERS):
+            sent(r_ref.at[step, pl.ds(0, outer - 1)], r_sem.at[step, 0])
+            sent(face_part(face_out, step), face_sem.at[step, 0])
+        sent(x_out.at[others_part], x_sem.at[0])
+        sent(q_out.at[others_part], q_sem.at[0])
+        sent(lam_out.at[others_part], lam_sem.at[0])
+
+
+def plane_finish(pre_ref, kph_ref, kpl_ref, q_ref, lam_ref, u_ref, lam_out):
+    high, low = split(q_ref[...])
+    columns = high.shape[0]
+    both = lax.dot_general(kph_ref[...], jnp.concatenate([high, low], axis=0), NT, preferred_element_type=F32)
+    both = both[:, :columns] + both[:, columns:]
+    u_ref[...] = pre_ref[...] - (both + lax.dot_general(kpl_ref[...], high, NT, preferred_element_type=F32))
+    lam_out[...] = lam_ref[...].T
+
+
+def size_of(buffers):
+    return sum((4 if kind == F32 else 2) * functools.reduce(lambda a, b: a * b, size) for size, kind in buffers)
+
+
+def plane_scratch(count, order, columns, owned, total, width, primal):
+    outer, inner = grid_of(count)
+    plane = 2 * inner
+    both = 2 * width
+    wide = lanes_of(primal)
+    span = lanes_of((plane + 1) * owned)
+    share = columns // plane
+    pairs = (plane + 2) * wide
+    return plane, [
+        ((order, columns), F32),
+        ((order, order), F32),
+        ((order, order), BF16),
+        ((order, order), BF16),
+        ((order, both + wide), BF16),
+        ((order, columns), BF16),
+        ((order, columns), BF16),
+        ((both + primal, order), F32),
+        ((plane, share, wide), F32),
+        ((plane, share, both), F32),
+        ((plane, share, wide), F32),
+        ((plane, share, both), F32),
+        ((plane + 3, owned, total), F32),
+        ((pairs, total), BF16),
+        ((pairs, total), BF16),
+        ((plane, primal, both), F32),
+        ((plane, primal, both), F32),
+        ((plane, 2, width, both), F32),
+        ((primal, width), F32),
+        ((primal, width), F32),
+        ((plane, wide, both), BF16),
+        ((plane, wide, both), BF16),
+        ((plane, wide, both), BF16),
+        ((plane, wide, both), BF16),
+        ((plane, both, both), BF16),
+        ((plane, both, both), BF16),
+        ((ITERS, outer, share, span), F32),
+        ((ITERS, 2, share, width), F32),
+        ((ITERS, 2, share, width), F32),
+        ((plane, share, both), F32),
+        ((plane, share, both), F32),
+        ((plane, share, wide), F32),
+        ((plane, share, wide), F32),
+        ((plane, share, width), F32),
+        ((plane, share, width), F32),
+    ]
+
+
+def planar(condensed, eigen_loads, coarse_inverse, face_rows, primal_rows, primal_slot):
+    count = lax.axis_size("sub")
+    order, columns = eigen_loads.shape
+    owned, total = coarse_inverse.shape
+    width = face_rows.shape[2]
+    primal = primal_rows.shape[1]
+    outer, inner = grid_of(count)
+    tile = 256 if order % 256 == 0 else order
+    tiles = order // tile
+    plane, buffers = plane_scratch(count, order, columns, owned, total, width, primal)
+    needed = size_of(buffers)
+    wide = lanes_of(primal)
+    dma = pltpu.SemaphoreType.DMA
+    vmem = pl.BlockSpec(memory_space=pltpu.VMEM)
+    shape = jax.ShapeDtypeStruct
+    held = [
+        pltpu.with_memory_space_constraint(value, pltpu.HBM)
+        for value in (face_rows, primal_rows, primal_slot, condensed, eigen_loads, coarse_inverse)
+    ]
+    parts = pl.pallas_call(
+        functools.partial(plane_kernel, count, primal, width),
+        out_shape=(
+            shape((order, columns), F32),
+            shape((order, wide), BF16),
+            shape((order, wide), BF16),
+            shape((columns, wide), F32),
+            shape((columns, width), F32),
+        ),
+        in_specs=[pl.BlockSpec(memory_space=pltpu.HBM)] * 6,
+        out_specs=(vmem,) * 5,
+        scratch_shapes=[
+            pltpu.SMEM(face_rows.shape, jnp.int32),
+            pltpu.SMEM(primal_rows.shape, jnp.int32),
+            pltpu.VMEM(face_rows.shape, jnp.int32),
+            pltpu.VMEM(primal_rows.shape, jnp.int32),
+            pltpu.VMEM(primal_slot.shape, jnp.int32),
+        ] + [pltpu.VMEM(size, kind) for size, kind in buffers] + [
+            dma((7,)),
+            dma((tiles,)),
+            dma((2,)),
+            dma((2,)),
+            dma(()),
+            dma((plane + 1,)),
+            dma(()),
+            dma((plane,)),
+            dma(()),
+            dma((plane,)),
+            dma(()),
+            dma((plane, 2)),
+            dma((2,)),
+            dma((4,)),
+            dma((3,)),
+            dma((ITERS, 2)),
+            dma((ITERS, 2)),
+            dma((2,)),
+            dma((2,)),
+            dma((2,)),
+        ],
+        compiler_params=pltpu.CompilerParams(
+            collective_id=0, has_side_effects=True, vmem_limit_bytes=min(PLANE_LIMIT, needed + needed // 3)
+        ),
+    )(*held)
+    return pl.pallas_call(
+        plane_finish,
+        out_shape=(shape((order, columns), F32), shape((width, columns), F32)),
+        in_specs=[vmem] * 5,
+        out_specs=(vmem, vmem),
+        compiler_params=pltpu.CompilerParams(vmem_limit_bytes=4 * order * columns * 8),
+    )(*parts)
+
+
+def fits_plane(condensed, eigen_loads, coarse_inverse, face_rows, primal_rows, primal_slot):
+    count = lax.axis_size("sub")
+    order, columns = eigen_loads.shape
+    owned, total = coarse_inverse.shape
+    width = face_rows.shape[2]
+    primal = primal_rows.shape[1]
+    outer, inner = grid_of(count)
+    plane = 2 * inner
+    if outer < 2 or columns % (8 * plane) or total % LANES or width % LANES or owned % 16 or primal != 2 * owned:
+        return False
+    _, buffers = plane_scratch(count, order, columns, owned, total, width, primal)
+    return size_of(buffers) <= PLANE_LIMIT * 3 // 4
+
+
+def local(*values):
+    return (planar if fits_plane(*values) else general)(*values)
+
+
+def general(condensed, eigen_loads, coarse_inverse, face_rows, primal_rows, primal_slot):
     count = lax.axis_size("sub")
     order, columns = eigen_loads.shape
     owned, total = coarse_inverse.shape

time: 51.8 us -> 45.4 us (0.88); the launches traced: 51 us -> 45.2 us
  Pallas kernels: 50.4 us -> 44.6 us
    pallas_call x2, Pallas kernels: 50.4 us -> 44.6 us  [the longest x1 43.2 us: planar(): pl.pallas_call(functools.partial(plane_kernel, count, primal, width), out...]
where the time goes in v1:
time: 45.4 us; the launch traced here: 45.2 us
  Pallas kernels  44.6 us (98%)
  between operations  0.64 us (1%)
    pallas_call x1, Pallas kernels, planar(): pl.pallas_call(functools.partial(plane_kernel, count, primal, width), out...  43.2 us
    pallas_call x1, Pallas kernels, planar(): pl.pallas_call(plane_finish, out_shape=(shape((order, columns), F32), sha...  1.36 us

profile of v1, /device:TPU:0, one launch (start us, length us, event | category | flops | bytes accessed | tf_op | source)
XLA Modules:
  0.0 45.2 jit_solution(17182453635091252695)
XLA Ops:
  0.6 43.2 %shard_map.77 = (f32[1536,128]{1,0:T(8,128)S(1)}, bf16[1536,128]{1,0:T(8,128)(2,1)S(1)}, bf16[1536,128]{1,0:T(8,128)(2,1)S(1)}, f32[128,128]{1,0:T(8,128)S(1)}, f32[128,128]{1,0:T(8,128)S(1)}) custom-call(s32[1,2,128]{2,1,0:T(2,128)} %face_hbm.1, s32[1,96]{1,0:T(1,128)} %prim_hbm.1, s32[1,96]{1,0:T(1,128)} %slot_hbm.1, f32[1536,1536]{1,0:T(8,128)} %k_hbm.1, ...), custom_call_target="tpu_custom_call" | custom-call | tf_op jit(solution)/shard_map/pallas_call | solution.py:879
  43.9 1.4 %shard_map.78 = (f32[1536,128]{1,0:T(8,128)}, f32[128,128]{1,0:T(8,128)}) custom-call(f32[1536,128]{1,0:T(8,128)S(1)} %get-tuple-element.7.pre_ref, bf16[1536,128]{1,0:T(8,128)(2,1)S(1)} %get-tuple-element.8.kph_ref, bf16[1536,128]{1,0:T(8,128)(2,1)S(1)} %get-tuple-element.9.kpl_ref, f32[128,128]{1,0:T(8,128)S(1)} %get-tuple-element.10.q_ref, ...), custom_call_target="tpu_custom_call" | custom-call | tf_op jit(solution)/shard_map/pallas_call | solution.py:922

commit v2 on v1

--- a/solution.py
+++ b/solution.py
@@ -363,7 +363,7 @@
 def plane_kernel(
     count, primal, width, face_hbm, prim_hbm, slot_hbm, k_hbm, f_hbm, cinv_hbm, pre_ref, kph_ref, kpl_ref, q_ref, lam_ref,
     face_s, prim_s, face_v, prim_v, slot_v, f_ref, k_ref, kh_ref, kl_ref, e_ref, fh_ref, fl_ref, ks_ref,
-    own_c, own_b, c_in, b_in, cinv_ref, cqh_ref, cql_ref, ac_ref, ap_ref, ar_ref, before_ref, after_ref,
+    own_c, own_b, c_in, b_in, cinv_ref, cqh_ref, cql_ref, ac_ref, ap_ref, ar_ref, edge_ref,
     ach_ref, acl_ref, aph_ref, apl_ref, arh_ref, arl_ref, r_ref, face_out, face_in, x_out, x_in, q_out, q_in, lam_out, lam_in,
     in_sem, k_sem, c_sem, b_sem, cinv_send, cinv_recv, ac_send, ac_recv, ap_send, ap_recv, ar_send, ar_recv,
     halo_send, halo_recv, edge_sem, r_sem, face_sem, x_sem, q_sem, lam_sem,
@@ -394,6 +394,11 @@
     mates = [at(z, other) for other in others]
     beyond = [at(lax.rem(z + m, outer), mine) for m in range(1, outer)]
     after, before = beyond[0], beyond[-1]
+    far_first = beyond[::-1]
+    if outer == 4:
+        end = lax.rem(z + 1, outer) < 2
+        mirror, skip, twin = outer - 1 - z, lax.rem(z + 2, outer), z + 1 - 2 * lax.rem(z, 2)
+        far_first = [at(place, mine) for place in (jnp.where(end, mirror, skip), jnp.where(end, skip, mirror), twin)]
 
     def remote(src, dst, ssem, rsem, peer):
         return pltpu.make_async_remote_copy(
@@ -465,15 +470,14 @@
         for peer in across_peers + [partner]:
             send(buf.at[own], buf.at[own], ssem, rsem.at[own], peer)
 
-    def relay(buf, ssem, rsem, shift=0):
+    def relay(buf, ssem, rsem):
         for other in across:
-            block = other + shift
-            arrived(buf.at[block], rsem.at[block])
-            send(buf.at[block], buf.at[block], ssem, rsem.at[block], partner)
-
-    def settle(buf, rsem, shift=0):
+            arrived(buf.at[other], rsem.at[other])
+            send(buf.at[other], buf.at[other], ssem, rsem.at[other], partner)
+
+    def settle(buf, rsem):
         for other in [mine] + across:
-            block = other + 1 - 2 * core + shift
+            block = other + 1 - 2 * core
             arrived(buf.at[block], rsem.at[block])
 
     with jax.named_scope("P_onehot"):
@@ -481,8 +485,46 @@
     with jax.named_scope("P_barrier"):
         pl.semaphore_wait(barrier, len(mates + beyond))
         cinv_copy.wait()
-    spread(cinv_ref, cinv_send, cinv_recv, mine + 1)
-
+    halves = owned // 2
+
+    def piece(block, half):
+        return cinv_ref.at[block, pl.ds(half * halves, halves)]
+
+    def send_far(half):
+        send(piece(1 + core, half), piece(plane + 1 + core, half), halo_send.at[0], halo_recv.at[0, half], before)
+
+    def send_near(half):
+        send(piece(plane, half), piece(0, half), halo_send.at[1], halo_recv.at[1, half], after)
+
+    def spread_coarse(half):
+        for peer in across_peers + [partner]:
+            rows = piece(mine + 1, half)
+            send(rows, rows, cinv_send, cinv_recv.at[mine + 1, half], peer)
+
+    def relay_coarse(half):
+        for other in across:
+            rows = piece(other + 1, half)
+            arrived(rows, cinv_recv.at[other + 1, half])
+            send(rows, rows, cinv_send, cinv_recv.at[other + 1, half], partner)
+        pl.when(mine >= 2)(functools.partial(send_far, half))
+        pl.when(mine == 1)(functools.partial(send_near, half))
+
+    def settle_coarse():
+        for half in range(2):
+            for other in [mine] + across:
+                block = other + 2 - 2 * core
+                arrived(piece(block, half), cinv_recv.at[block, half])
+
+    def last_edge():
+        send(ac_ref.at[plane - 1, :, pl.ds(0, width)], edge_ref.at[0], edge_sem.at[0], edge_sem.at[1], after)
+
+    def first_edge():
+        send(ac_ref.at[0, :, pl.ds(width, width)], edge_ref.at[1], edge_sem.at[0], edge_sem.at[1], before)
+
+    spread_coarse(0)
+    for half in range(2):
+        pl.when(mine < 2)(functools.partial(send_far, half))
+        pl.when(mine == plane - 1)(functools.partial(send_near, half))
     with jax.named_scope("P_f"):
         f_copy.wait()
         high, low = split(f_ref[...])
@@ -512,21 +554,18 @@
         high, low = split(ks_ref[rows, :])
         return product_parts(high, low, fh_ref[...], fl_ref[...])
 
-    with jax.named_scope("P_first"):
-        picked(both, primal, lambda i: prim_s[0, i])
-        own_c[...] = in_order(first(slice(both, both + primal))).T.reshape(own_c.shape)
+    def columns_of(rows, picks):
+        high, low = split(ks_ref[rows, :])
+        return jnp.dot(high, picks, preferred_element_type=F32) + jnp.dot(low, picks, preferred_element_type=F32)
+
+    def give(out, into, sems):
         for other, peer in zip(others, mates):
-            send(own_c.at[other], c_in.at[mine], c_sem.at[0], c_sem.at[1], peer)
-        c_in[mine] = own_c[mine]
-    with jax.named_scope("P_firstb"):
-        picked(0, width, lambda i: face_s[0, 1, i])
-        picked(width, width, lambda i: face_s[0, 0, i])
-        loads = first(slice(0, both))
-        own_b[:, :, :width] = loads[:width].T.reshape(plane, share, width)
-        own_b[:, :, width:] = loads[width:].T.reshape(plane, share, width)
-        for other, peer in zip(others, mates):
-            send(own_b.at[other], b_in.at[mine], b_sem.at[0], b_sem.at[1], peer)
-        b_in[mine] = own_b[mine]
+            send(out.at[other], into.at[mine], sems.at[0], sems.at[1], peer)
+        into[mine] = out[mine]
+
+    def taken(into, sems):
+        arrived(into.at[pl.ds(0, plane - 1)], sems.at[1])
+
     def assembled(parts):
         sums = None
         for i, part in enumerate(parts):
@@ -537,7 +576,7 @@
 
     def publish(step, parts):
         r_ref[step, z] = assembled(parts)
-        for peer in reversed(beyond):
+        for peer in far_first:
             rows = r_ref.at[step, z]
             send(rows, rows, r_sem.at[step, 0], r_sem.at[step, 1], peer)
 
@@ -551,58 +590,6 @@
     def face_part(ref, step):
         return ref.at[step] if step + 1 < ITERS else ref.at[step, pl.ds(0, 1)]
 
-    def columns_of(rows, picks):
-        high, low = split(ks_ref[rows, :])
-        return jnp.dot(high, picks, preferred_element_type=F32) + jnp.dot(low, picks, preferred_element_type=F32)
-
-    def primal_columns(first_tile, last_tile):
-        picks = e_ref[:, both:]
-
-        @pl.loop(first_tile, last_tile)
-        def _(c):
-            rows = pl.ds(pl.multiple_of(c * tile, tile), tile)
-            kph_ref[rows, :] = jnp.dot(kh_ref[rows, :], picks, preferred_element_type=F32).astype(BF16)
-            kpl_ref[rows, :] = jnp.dot(kl_ref[rows, :], picks, preferred_element_type=F32).astype(BF16)
-
-    def coarse_rows(blocks):
-        for b in blocks:
-            high, low = split(cinv_ref[b])
-            for pair, half in ((b, 0), (b - 1, 1)):
-                if 0 <= pair < plane + 2:
-                    start = pair * wide + half * owned
-                    cqh_ref[start:start + owned, :] = high
-                    cql_ref[start:start + owned, :] = low
-
-    def halves_of(refs, src):
-        for i in range(plane):
-            for ref, part in zip(refs, split(src[i])):
-                ref[i, :primal, :] = part
-                ref[i, primal:, :] = jnp.zeros((wide - primal, both), BF16)
-
-    with jax.named_scope("P_ac"):
-        found = columns_of(slice(0, both), e_ref[:, both:])
-        ac_ref[mine, :, :width] = found[:width].T[:primal]
-        ac_ref[mine, :, width:] = found[width:].T[:primal]
-        spread(ac_ref, ac_send, ac_recv, mine)
-    with jax.named_scope("P_relayc"):
-        relay(cinv_ref, cinv_send, cinv_recv, 1)
-    with jax.named_scope("P_cwait"):
-        arrived(c_in.at[pl.ds(0, plane - 1)], c_sem.at[1])
-    publish(0, [c_in[i] for i in range(plane)])
-    with jax.named_scope("P_ap"):
-        ap_ref[mine] = in_order(columns_of(slice(both, both + primal), e_ref[:, :both]))[:primal]
-        spread(ap_ref, ap_send, ap_recv, mine)
-    with jax.named_scope("P_halo"):
-        settle(cinv_ref, cinv_recv, 1)
-        halves = owned // 2
-        near = cinv_ref.at[0, pl.ds(core * halves, halves)]
-        far = cinv_ref.at[plane + 1 + core]
-        send(cinv_ref.at[1 + core], far, halo_send.at[0], halo_recv.at[0], before)
-        send(cinv_ref.at[plane, pl.ds(core * halves, halves)], near, halo_send.at[1], halo_recv.at[1], after)
-    with jax.named_scope("P_bwait"):
-        arrived(b_in.at[pl.ds(0, plane - 1)], b_sem.at[1])
-    faces(0, b_in[plane - 1, :, :width], b_in[0, :, width:])
-
     urgent = jnp.where(mine == 0, 1, 0)
 
     def spread_half(half):
@@ -623,40 +610,110 @@
             half = jnp.where(block == 0, 1 - flip, flip)
             arrived(ar_ref.at[block, half], ar_recv.at[block, half])
 
+    with jax.named_scope("P_first"):
+        picked(both, primal, lambda i: prim_s[0, i])
+        own_c[...] = in_order(first(slice(both, both + primal))).T.reshape(own_c.shape)
+        give(own_c, c_in, c_sem)
+    spread_coarse(1)
+    with jax.named_scope("P_pick"):
+        picked(0, width, lambda i: face_s[0, 1, i])
+        picked(width, width, lambda i: face_s[0, 0, i])
+    with jax.named_scope("P_ac"):
+        found = columns_of(slice(0, both), e_ref[:, both:])
+        ac_ref[mine, :, :width] = found[:width].T[:primal]
+        ac_ref[mine, :, width:] = found[width:].T[:primal]
+        spread(ac_ref, ac_send, ac_recv, mine)
+    with jax.named_scope("P_relayc0"):
+        relay_coarse(0)
+    with jax.named_scope("P_cwait"):
+        taken(c_in, c_sem)
+    publish(0, [c_in[i] for i in range(plane)])
+    pl.when(mine == plane - 1)(last_edge)
+    pl.when(mine == 0)(first_edge)
+    with jax.named_scope("P_firstb"):
+        loads = first(slice(0, both))
+        own_b[:, :, :width] = loads[:width].T.reshape(plane, share, width)
+        own_b[:, :, width:] = loads[width:].T.reshape(plane, share, width)
+        give(own_b, b_in, b_sem)
+    with jax.named_scope("P_relayc1"):
+        relay_coarse(1)
+    with jax.named_scope("P_ap"):
+        ap_ref[mine] = in_order(columns_of(slice(both, both + primal), e_ref[:, :both]))[:primal]
+        spread(ap_ref, ap_send, ap_recv, mine)
     with jax.named_scope("P_ar"):
         found = columns_of(slice(0, both), e_ref[:, :both])
         ar_ref[mine, 0] = found[:width]
         ar_ref[mine, 1] = found[width:]
+        spread_half(urgent)
+        spread_half(1 - urgent)
+    with jax.named_scope("P_relayac"):
+        relay(ac_ref, ac_send, ac_recv)
+    pl.when(mine == 1)(last_edge)
+    pl.when(mine == 2)(first_edge)
+    with jax.named_scope("P_bwait"):
+        taken(b_in, b_sem)
+    faces(0, b_in[plane - 1, :, :width], b_in[0, :, width:])
     with jax.named_scope("P_halve"):
         halve(0, tiles)
+
+    def primal_columns(first_tile, last_tile):
+        picks = e_ref[:, both:]
+
+        @pl.loop(first_tile, last_tile)
+        def _(c):
+            rows = pl.ds(pl.multiple_of(c * tile, tile), tile)
+            kph_ref[rows, :] = jnp.dot(kh_ref[rows, :], picks, preferred_element_type=F32).astype(BF16)
+            kpl_ref[rows, :] = jnp.dot(kl_ref[rows, :], picks, preferred_element_type=F32).astype(BF16)
+
+    def coarse_rows(first_block, last_block):
+        for b in range(first_block, last_block):
+            for ref, part in zip((cqh_ref, cql_ref), split(cinv_ref[b])):
+                ref[b * owned:(b + 1) * owned, :] = part
+
+    def halves_of(refs, src):
+        for i in range(plane):
+            for ref, part in zip(refs, split(src[i])):
+                ref[i, :primal, :] = part
+                ref[i, primal:, :] = jnp.zeros((wide - primal, both), BF16)
+
+    early = tiles // 3
+    with jax.named_scope("P_halo"):
+        settle_coarse()
+        far = cinv_ref.at[plane + 1 + core]
+        near = cinv_ref.at[0]
+        for half in range(2):
+            arrived(piece(plane + 1 + core, half), halo_recv.at[0, half])
+        send(far, far, halo_send.at[0], halo_recv.at[2, 0], partner)
+
+        @pl.when(core == 1)
+        def _():
+            for half in range(2):
+                arrived(piece(0, half), halo_recv.at[1, half])
+            send(near, near, halo_send.at[1], halo_recv.at[2, 1], partner)
+
     with jax.named_scope("P_cq"):
+        rest = (plane + 3) * owned
         for ref in (cqh_ref, cql_ref):
-            for pair in range(plane + 2):
-                ref[pair * wide + primal:(pair + 1) * wide, :] = jnp.zeros((wide - primal, total), BF16)
-        coarse_rows(range(1, plane + 1))
-    with jax.named_scope("P_relayac"):
-        relay(ac_ref, ac_send, ac_recv)
-        spread_half(urgent)
+            ref[rest:, :] = jnp.zeros((ref.shape[0] - rest, total), BF16)
+        coarse_rows(1, plane + 1)
     with jax.named_scope("P_settleac"):
         settle(ac_ref, ac_recv)
-        send(ac_ref.at[plane - 1, :, pl.ds(0, width)], before_ref, edge_sem.at[0], edge_sem.at[1], after)
-        send(ac_ref.at[0, :, pl.ds(width, width)], after_ref, edge_sem.at[0], edge_sem.at[2], before)
         halves_of((ach_ref, acl_ref), ac_ref)
-    with jax.named_scope("P_halo2"):
-        arrived(far, halo_recv.at[0])
-        send(far, far, halo_send.at[0], halo_recv.at[2], partner)
-        arrived(near, halo_recv.at[1])
-        send(near, near, halo_send.at[1], halo_recv.at[3], partner)
     with jax.named_scope("P_relayap"):
         relay(ap_ref, ap_send, ap_recv)
-        spread_half(1 - urgent)
-    half_tiles = tiles // 2
-    with jax.named_scope("P_halo3"):
-        other_near = cinv_ref.at[0, pl.ds((1 - core) * halves, halves)]
-        other_far = cinv_ref.at[plane + 2 - core]
-        arrived(other_far, halo_recv.at[2])
-        arrived(other_near, halo_recv.at[3])
-        coarse_rows([0, plane + 1, plane + 2])
+    with jax.named_scope("P_halo2"):
+        arrived(cinv_ref.at[plane + 2 - core], halo_recv.at[2, 0])
+
+        @pl.when(core == 0)
+        def _():
+            arrived(near, halo_recv.at[2, 1])
+
+        coarse_rows(0, 1)
+        coarse_rows(plane + 1, plane + 3)
+    with jax.named_scope("P_edge0"):
+        rows = edge_ref.at[1 - core]
+        arrived(rows, edge_sem.at[1])
+        send(rows, rows, edge_sem.at[3], edge_sem.at[2], partner)
 
     def uncorrected(first_tile, last_tile):
         @pl.loop(first_tile, last_tile)
@@ -681,11 +738,13 @@
     edges = None
     for step in range(ITERS):
         if step == ITERS - 1:
+            with jax.named_scope("P_primcol1"):
+                primal_columns(tiles - early, tiles)
             with jax.named_scope("P_xwait"):
                 arrived(x_in.at[pl.ds(0, plane - 1)], x_sem.at[1])
                 changed_loads()
             with jax.named_scope("P_uncorr0"):
-                uncorrected(0, half_tiles)
+                uncorrected(0, early)
         with jax.named_scope(f"P_rwait{step}"):
             arrived(r_ref.at[step, pl.ds(0, outer - 1)], r_sem.at[step, 1])
         with jax.named_scope(f"P_coarse{step}"):
@@ -695,7 +754,9 @@
                 part = pltpu.roll(part, plane * owned * i, 1) if i else part
                 sums = part if sums is None else sums + part
             coarse = tall(sums, cqh_ref[...], cql_ref[...], NT)
-            steps = [coarse[:, i * wide:(i + 1) * wide] for i in range(plane + 2)]
+            steps = [coarse[:, :wide]]
+            for i in range(1, plane + 2):
+                steps.append(pltpu.roll(coarse, coarse.shape[1] - owned * i, 1)[:, :wide])
             if step == ITERS - 1:
                 for i in range(plane):
                     q_out[i] = steps[i + 1]
@@ -704,9 +765,8 @@
                 q_in[mine] = q_out[mine]
         if edges is None:
             with jax.named_scope("P_edge"):
-                arrived(before_ref, edge_sem.at[1])
-                arrived(after_ref, edge_sem.at[2])
-                edges = [split(padded(ref[...])) for ref in (before_ref, after_ref)]
+                arrived(edge_ref.at[core], edge_sem.at[2])
+                edges = [split(padded(edge_ref[i])) for i in range(2)]
         with jax.named_scope(f"P_faces{step}"):
             arrived(face_part(face_in, step), face_sem.at[step, 1])
         with jax.named_scope(f"P_update{step}"):
@@ -752,12 +812,12 @@
                 last_right = tall(changes[-1], arh_ref[plane - 1, :width], arl_ref[plane - 1, :width], NT)
                 first_left = tall(changes[0], arh_ref[0, width:], arl_ref[0, width:], NT)
                 faces(1, b_in[plane - 1, :, :width] + last_right, b_in[0, :, width:] + first_left)
-            with jax.named_scope("P_primcol"):
-                primal_columns(0, half_tiles)
+            with jax.named_scope("P_primcol0"):
+                primal_columns(0, early)
             with jax.named_scope("P_relayr1"):
                 relay_half(1)
-            with jax.named_scope("P_primcol"):
-                primal_columns(half_tiles, tiles)
+            with jax.named_scope("P_primcol0"):
+                primal_columns(early, tiles - early)
             with jax.named_scope("P_settler1"):
                 settle_half(1)
                 for i in range(plane):
@@ -772,7 +832,7 @@
                 faces(step + 1, values[plane - 1][:, :width], values[0][:, width:])
 
     with jax.named_scope("P_uncorr1"):
-        uncorrected(half_tiles, tiles)
+        uncorrected(early, tiles)
     with jax.named_scope("P_qwait"):
         arrived(q_in.at[pl.ds(0, plane - 1)], q_sem.at[1])
         q_ref[...] = q_in[...].reshape(q_ref.shape)
@@ -787,8 +847,13 @@
         for ref, sem in ((ac_ref, ac_send), (ap_ref, ap_send), (ar_ref, ar_send)):
             sent(ref.at[others_part], sem)
         sent(cinv_ref.at[pl.ds(0, 2)], halo_send.at[0])
-        sent(cinv_ref.at[0], halo_send.at[1])
-        sent(ac_ref.at[0], edge_sem.at[0])
+
+        @pl.when(core == 1)
+        def _():
+            sent(cinv_ref.at[pl.ds(0, 2)], halo_send.at[1])
+
+        sent(edge_ref.at[0], edge_sem.at[0])
+        sent(edge_ref.at[0], edge_sem.at[3])
         for step in range(ITERS):
             sent(r_ref.at[step, pl.ds(0, outer - 1)], r_sem.at[step, 0])
             sent(face_part(face_out, step), face_sem.at[step, 0])
@@ -797,13 +862,26 @@
         sent(lam_out.at[others_part], lam_sem.at[0])
 
 
-def plane_finish(pre_ref, kph_ref, kpl_ref, q_ref, lam_ref, u_ref, lam_out):
+def plane_finish(pre_ref, kph_ref, kpl_ref, q_ref, lam_ref, u_hbm, lam_hbm, u_ref, lam_out, sem):
+    tiles = sem.shape[0] - 1
+    tile = u_ref.shape[0] // tiles
+    columns = q_ref.shape[0]
+    lam_out[...] = lam_ref[...].T
+    copies = [pltpu.make_async_copy(lam_out, lam_hbm, sem.at[tiles])]
+    copies[0].start()
     high, low = split(q_ref[...])
-    columns = high.shape[0]
-    both = lax.dot_general(kph_ref[...], jnp.concatenate([high, low], axis=0), NT, preferred_element_type=F32)
-    both = both[:, :columns] + both[:, columns:]
-    u_ref[...] = pre_ref[...] - (both + lax.dot_general(kpl_ref[...], high, NT, preferred_element_type=F32))
-    lam_out[...] = lam_ref[...].T
+    pair = jnp.concatenate([high, low], axis=0)
+    for c in range(tiles):
+        rows = pl.ds(c * tile, tile)
+        both = lax.dot_general(kph_ref[rows, :], pair, NT, preferred_element_type=F32)
+        both = both[:, :columns] + both[:, columns:]
+        u_ref[rows, :] = pre_ref[rows, :] - (
+            both + lax.dot_general(kpl_ref[rows, :], high, NT, preferred_element_type=F32)
+        )
+        copies.append(pltpu.make_async_copy(u_ref.at[rows, :], u_hbm.at[rows, :], sem.at[c]))
+        copies[-1].start()
+    for copy in copies:
+        copy.wait()
 
 
 def size_of(buffers):
@@ -817,7 +895,7 @@
     wide = lanes_of(primal)
     span = lanes_of((plane + 1) * owned)
     share = columns // plane
-    pairs = (plane + 2) * wide
+    pairs = lanes_of((plane + 3) * owned)
     return plane, [
         ((order, columns), F32),
         ((order, order), F32),
@@ -837,8 +915,7 @@
         ((plane, primal, both), F32),
         ((plane, primal, both), F32),
         ((plane, 2, width, both), F32),
-        ((primal, width), F32),
-        ((primal, width), F32),
+        ((2, primal, width), F32),
         ((plane, wide, both), BF16),
         ((plane, wide, both), BF16),
         ((plane, wide, both), BF16),
@@ -866,6 +943,7 @@
     outer, inner = grid_of(count)
     tile = 256 if order % 256 == 0 else order
     tiles = order // tile
+    pieces = tiles // 2 if tiles % 2 == 0 else 1
     plane, buffers = plane_scratch(count, order, columns, owned, total, width, primal)
     needed = size_of(buffers)
     wide = lanes_of(primal)
@@ -899,7 +977,7 @@
             dma((2,)),
             dma((2,)),
             dma(()),
-            dma((plane + 1,)),
+            dma((plane + 1, 2)),
             dma(()),
             dma((plane,)),
             dma(()),
@@ -907,8 +985,8 @@
             dma(()),
             dma((plane, 2)),
             dma((2,)),
+            dma((3, 2)),
             dma((4,)),
-            dma((3,)),
             dma((ITERS, 2)),
             dma((ITERS, 2)),
             dma((2,)),
@@ -923,7 +1001,8 @@
         plane_finish,
         out_shape=(shape((order, columns), F32), shape((width, columns), F32)),
         in_specs=[vmem] * 5,
-        out_specs=(vmem, vmem),
+        out_specs=(pl.BlockSpec(memory_space=pltpu.HBM),) * 2,
+        scratch_shapes=[pltpu.VMEM((order, columns), F32), pltpu.VMEM((width, columns), F32), dma((pieces + 1,))],
         compiler_params=pltpu.CompilerParams(vmem_limit_bytes=4 * order * columns * 8),
     )(*parts)
 
@@ -936,7 +1015,7 @@
     primal = primal_rows.shape[1]
     outer, inner = grid_of(count)
     plane = 2 * inner
-    if outer < 2 or columns % (8 * plane) or total % LANES or width % LANES or owned % 16 or primal != 2 * owned:
+    if outer < 2 or inner != 2 or columns % (8 * plane) or total % LANES or width % LANES or owned % 16 or primal != 2 * owned:
         return False
     _, buffers = plane_scratch(count, order, columns, owned, total, width, primal)
     return size_of(buffers) <= PLANE_LIMIT * 3 // 4

time: 45.4 us -> 38.8 us (0.85)
  Pallas kernels: 44.6 us -> 38 us
    pallas_call x1, Pallas kernels: 43.2 us -> 36.7 us  [planar(): pl.pallas_call(functools.partial(plane_kernel, count, primal, width), out...]
where the time goes in v2:
time: 38.8 us; the launch traced here: 38.6 us
  Pallas kernels  38 us (98%)
  between operations  0.64 us (2%)
    pallas_call x1, Pallas kernels, planar(): pl.pallas_call(functools.partial(plane_kernel, count, primal, width), out...  36.7 us
    pallas_call x1, Pallas kernels, planar(): pl.pallas_call(plane_finish, out_shape=(shape((order, columns), F32), sha...  1.24 us

profile of v2, /device:TPU:0, one launch (start us, length us, event | category | flops | bytes accessed | tf_op | source)
XLA Modules:
  0.0 38.6 jit_solution(10879617304408969740)
XLA Ops:
  0.6 36.7 %shard_map.77 = (f32[1536,128]{1,0:T(8,128)S(1)}, bf16[1536,128]{1,0:T(8,128)(2,1)S(1)}, bf16[1536,128]{1,0:T(8,128)(2,1)S(1)}, f32[128,128]{1,0:T(8,128)S(1)}, f32[128,128]{1,0:T(8,128)S(1)}) custom-call(s32[1,2,128]{2,1,0:T(2,128)} %face_hbm.1, s32[1,96]{1,0:T(1,128)} %prim_hbm.1, s32[1,96]{1,0:T(1,128)} %slot_hbm.1, f32[1536,1536]{1,0:T(8,128)} %k_hbm.1, ...), custom_call_target="tpu_custom_call" | custom-call | tf_op jit(solution)/shard_map/pallas_call | solution.py:957
  37.4 1.2 %shard_map.78 = (f32[1536,128]{1,0:T(8,128)}, f32[128,128]{1,0:T(8,128)}) custom-call(f32[1536,128]{1,0:T(8,128)S(1)} %get-tuple-element.7.pre_ref, bf16[1536,128]{1,0:T(8,128)(2,1)S(1)} %get-tuple-element.8.kph_ref, bf16[1536,128]{1,0:T(8,128)(2,1)S(1)} %get-tuple-element.9.kpl_ref, f32[128,128]{1,0:T(8,128)S(1)} %get-tuple-element.10.q_ref, ...), custom_call_target="tpu_custom_call" | custom-call | tf_op jit(solution)/shard_map/pallas_call | solution.py:1000

commit v3 on v2

--- a/solution.py
+++ b/solution.py
@@ -361,8 +361,8 @@
 
 
 def plane_kernel(
-    count, primal, width, face_hbm, prim_hbm, slot_hbm, k_hbm, f_hbm, cinv_hbm, pre_ref, kph_ref, kpl_ref, q_ref, lam_ref,
-    face_s, prim_s, face_v, prim_v, slot_v, f_ref, k_ref, kh_ref, kl_ref, e_ref, fh_ref, fl_ref, ks_ref,
+    count, primal, width, face_hbm, prim_hbm, slot_hbm, k_hbm, f_hbm, cinv_hbm, u_ref, lam_ref,
+    face_s, prim_s, face_v, prim_v, slot_v, f_ref, k_ref, kh_ref, kl_ref, kph_ref, kpl_ref, e_ref, fh_ref, fl_ref, ks_ref,
     own_c, own_b, c_in, b_in, cinv_ref, cqh_ref, cql_ref, ac_ref, ap_ref, ar_ref, edge_ref,
     ach_ref, acl_ref, aph_ref, apl_ref, arh_ref, arl_ref, r_ref, face_out, face_in, x_out, x_in, q_out, q_in, lam_out, lam_in,
     in_sem, k_sem, c_sem, b_sem, cinv_send, cinv_recv, ac_send, ac_recv, ap_send, ap_recv, ar_send, ar_recv,
@@ -392,13 +392,24 @@
     across_peers = [at(z, other) for other in across]
     others = [lax.rem(mine + m, plane) for m in range(1, plane)]
     mates = [at(z, other) for other in others]
-    beyond = [at(lax.rem(z + m, outer), mine) for m in range(1, outer)]
-    after, before = beyond[0], beyond[-1]
+    turned = lax.rem(z, 2) if outer % 2 == 0 else 0
+
+    def swapped(index, turn):
+        return index + turn * (1 - 2 * lax.rem(index, 2))
+
+    portion = swapped(mine, turned)
+
+    def kin(place):
+        return at(place, swapped(portion, lax.rem(place, 2) if outer % 2 == 0 else 0))
+
+    beyond = [kin(lax.rem(z + m, outer)) for m in range(1, outer)]
+    next_kin, last_kin = beyond[0], beyond[-1]
+    after, before = [at(lax.rem(z + m, outer), mine) for m in (1, outer - 1)]
     far_first = beyond[::-1]
     if outer == 4:
         end = lax.rem(z + 1, outer) < 2
         mirror, skip, twin = outer - 1 - z, lax.rem(z + 2, outer), z + 1 - 2 * lax.rem(z, 2)
-        far_first = [at(place, mine) for place in (jnp.where(end, mirror, skip), jnp.where(end, skip, mirror), twin)]
+        far_first = [kin(place) for place in (jnp.where(end, mirror, skip), jnp.where(end, skip, mirror), twin)]
 
     def remote(src, dst, ssem, rsem, peer):
         return pltpu.make_async_remote_copy(
@@ -433,7 +444,8 @@
         k_copy(c).start()
 
     barrier = pltpu.get_barrier_semaphore()
-    for peer in mates + beyond:
+    greeted = mates + beyond + ([after, before] if outer % 2 == 0 else [])
+    for peer in greeted:
         pl.semaphore_signal(barrier, inc=1, device_id={"sub": peer}, device_id_type=MESH)
 
     with jax.named_scope("P_ints"):
@@ -483,7 +495,7 @@
     with jax.named_scope("P_onehot"):
         one_hot_columns()
     with jax.named_scope("P_barrier"):
-        pl.semaphore_wait(barrier, len(mates + beyond))
+        pl.semaphore_wait(barrier, len(greeted))
         cinv_copy.wait()
     halves = owned // 2
 
@@ -560,8 +572,13 @@
 
     def give(out, into, sems):
         for other, peer in zip(others, mates):
-            send(out.at[other], into.at[mine], sems.at[0], sems.at[1], peer)
-        into[mine] = out[mine]
+            send(out.at[swapped(other, turned)], into.at[mine], sems.at[0], sems.at[1], peer)
+        into[mine] = out[portion]
+
+    def give_back(out, into, sems):
+        for other, peer in zip(others, mates):
+            send(out.at[other], into.at[portion], sems.at[0], sems.at[1], peer)
+        into[portion] = out[mine]
 
     def taken(into, sems):
         arrived(into.at[pl.ds(0, plane - 1)], sems.at[1])
@@ -582,10 +599,10 @@
 
     def faces(step, last_right, first_left):
         face_out[step, 0] = first_left
-        send(face_out.at[step, 0], face_in.at[step, 0], face_sem.at[step, 0], face_sem.at[step, 1], before)
+        send(face_out.at[step, 0], face_in.at[step, 0], face_sem.at[step, 0], face_sem.at[step, 1], last_kin)
         if step + 1 < ITERS:
             face_out[step, 1] = last_right
-            send(face_out.at[step, 1], face_in.at[step, 1], face_sem.at[step, 0], face_sem.at[step, 1], after)
+            send(face_out.at[step, 1], face_in.at[step, 1], face_sem.at[step, 0], face_sem.at[step, 1], next_kin)
 
     def face_part(ref, step):
         return ref.at[step] if step + 1 < ITERS else ref.at[step, pl.ds(0, 1)]
@@ -665,10 +682,11 @@
             kph_ref[rows, :] = jnp.dot(kh_ref[rows, :], picks, preferred_element_type=F32).astype(BF16)
             kpl_ref[rows, :] = jnp.dot(kl_ref[rows, :], picks, preferred_element_type=F32).astype(BF16)
 
-    def coarse_rows(first_block, last_block):
-        for b in range(first_block, last_block):
-            for ref, part in zip((cqh_ref, cql_ref), split(cinv_ref[b])):
-                ref[b * owned:(b + 1) * owned, :] = part
+    last_row = cqh_ref.shape[0]
+
+    def coarse_rows(block, start):
+        for ref, part in zip((cqh_ref, cql_ref), split(cinv_ref[block])):
+            ref[start:start + owned, :] = part
 
     def halves_of(refs, src):
         for i in range(plane):
@@ -677,13 +695,14 @@
                 ref[i, primal:, :] = jnp.zeros((wide - primal, both), BF16)
 
     early = tiles // 3
+    sooner = jnp.where(mine < 2, early // 2, early)
     with jax.named_scope("P_halo"):
         settle_coarse()
-        far = cinv_ref.at[plane + 1 + core]
         near = cinv_ref.at[0]
         for half in range(2):
-            arrived(piece(plane + 1 + core, half), halo_recv.at[0, half])
-        send(far, far, halo_send.at[0], halo_recv.at[2, 0], partner)
+            rows = piece(plane + 1 + core, half)
+            arrived(rows, halo_recv.at[0, half])
+            send(rows, rows, halo_send.at[0], halo_recv.at[3, half], partner)
 
         @pl.when(core == 1)
         def _():
@@ -692,34 +711,36 @@
             send(near, near, halo_send.at[1], halo_recv.at[2, 1], partner)
 
     with jax.named_scope("P_cq"):
-        rest = (plane + 3) * owned
         for ref in (cqh_ref, cql_ref):
-            ref[rest:, :] = jnp.zeros((ref.shape[0] - rest, total), BF16)
-        coarse_rows(1, plane + 1)
+            ref[plane * owned:, :] = jnp.zeros((last_row - plane * owned, total), BF16)
+        for i in range(plane):
+            coarse_rows(i + 1, i * owned)
     with jax.named_scope("P_settleac"):
         settle(ac_ref, ac_recv)
         halves_of((ach_ref, acl_ref), ac_ref)
-    with jax.named_scope("P_relayap"):
-        relay(ap_ref, ap_send, ap_recv)
-    with jax.named_scope("P_halo2"):
-        arrived(cinv_ref.at[plane + 2 - core], halo_recv.at[2, 0])
-
-        @pl.when(core == 0)
-        def _():
-            arrived(near, halo_recv.at[2, 1])
-
-        coarse_rows(0, 1)
-        coarse_rows(plane + 1, plane + 3)
     with jax.named_scope("P_edge0"):
         rows = edge_ref.at[1 - core]
         arrived(rows, edge_sem.at[1])
         send(rows, rows, edge_sem.at[3], edge_sem.at[2], partner)
+    with jax.named_scope("P_relayap"):
+        relay(ap_ref, ap_send, ap_recv)
+    def coarse_halos():
+        for half in range(2):
+            arrived(piece(plane + 2 - core, half), halo_recv.at[3, half])
+
+        @pl.when(core == 0)
+        def _():
+            arrived(near, halo_recv.at[2, 1])
+
+        coarse_rows(plane + 1, plane * owned)
+        coarse_rows(plane + 2, (plane + 1) * owned)
+        coarse_rows(0, last_row - owned)
 
     def uncorrected(first_tile, last_tile):
         @pl.loop(first_tile, last_tile)
         def _(c):
             rows = pl.ds(pl.multiple_of(c * tile, tile), tile)
-            pre_ref[rows, :] = product_parts(kh_ref[rows, :], kl_ref[rows, :], fh_ref[...], fl_ref[...])
+            u_ref[rows, :] = product_parts(kh_ref[rows, :], kl_ref[rows, :], fh_ref[...], fl_ref[...])
 
     def changed_loads():
         high, low = split(x_in[...].reshape(columns, both))
@@ -729,6 +750,10 @@
         high, low = split(f_ref[...] + (moved[:, :columns] + moved[:, columns:]))
         fh_ref[...] = high
         fl_ref[...] = low
+
+    def shifted(value, block):
+        return (pltpu.roll(value, value.shape[1] - owned * block, 1) if block > 0 else pltpu.roll(
+            value, owned, 1) if block else value)[:, :wide]
 
     def padded(value):
         return jnp.concatenate([value, jnp.zeros((wide - primal, value.shape[1]), F32)], axis=0)
@@ -744,7 +769,7 @@
                 arrived(x_in.at[pl.ds(0, plane - 1)], x_sem.at[1])
                 changed_loads()
             with jax.named_scope("P_uncorr0"):
-                uncorrected(0, early)
+                uncorrected(0, sooner)
         with jax.named_scope(f"P_rwait{step}"):
             arrived(r_ref.at[step, pl.ds(0, outer - 1)], r_sem.at[step, 1])
         with jax.named_scope(f"P_coarse{step}"):
@@ -753,16 +778,22 @@
                 part = jnp.concatenate([r_ref[step, i], jnp.zeros((share, total - span), F32)], axis=1)
                 part = pltpu.roll(part, plane * owned * i, 1) if i else part
                 sums = part if sums is None else sums + part
-            coarse = tall(sums, cqh_ref[...], cql_ref[...], NT)
-            steps = [coarse[:, :wide]]
-            for i in range(1, plane + 2):
-                steps.append(pltpu.roll(coarse, coarse.shape[1] - owned * i, 1)[:, :wide])
+            if step:
+                coarse = tall(sums, cqh_ref[...], cql_ref[...], NT)
+                moved = []
+            else:
+                own = tall(sums, cqh_ref[:lanes_of(plane * owned)], cql_ref[:lanes_of(plane * owned)], NT)
+                moved = [values[i] - tall(shifted(own, i), ach_ref[i], acl_ref[i], NN) for i in range(plane - 1)]
+                with jax.named_scope("P_halo2"):
+                    coarse_halos()
+                low_row = (plane - 1) * owned // LANES * LANES
+                rest = tall(sums, cqh_ref[low_row:], cql_ref[low_row:], NT)
+                coarse = jnp.concatenate([own[:, :low_row], rest], axis=1)
+            steps = [shifted(coarse, i - 1) for i in range(plane + 2)]
             if step == ITERS - 1:
                 for i in range(plane):
                     q_out[i] = steps[i + 1]
-                for other, peer in zip(others, mates):
-                    send(q_out.at[other], q_in.at[mine], q_sem.at[0], q_sem.at[1], peer)
-                q_in[mine] = q_out[mine]
+                give_back(q_out, q_in, q_sem)
         if edges is None:
             with jax.named_scope("P_edge"):
                 arrived(edge_ref.at[core], edge_sem.at[2])
@@ -770,7 +801,7 @@
         with jax.named_scope(f"P_faces{step}"):
             arrived(face_part(face_in, step), face_sem.at[step, 1])
         with jax.named_scope(f"P_update{step}"):
-            moved = [values[i] - tall(steps[i + 1], ach_ref[i], acl_ref[i], NN) for i in range(plane)]
+            moved += [values[i] - tall(steps[i + 1], ach_ref[i], acl_ref[i], NN) for i in range(len(moved), plane)]
             right = [part[:, :width] for part in moved]
             left = [part[:, width:] for part in moved]
             left.append(face_in[step, 0] - tall(steps[plane + 1], *edges[1], NN))
@@ -781,9 +812,7 @@
             else:
                 for i in range(plane):
                     lam_out[i] = lam_next[i]
-                for other, peer in zip(others, mates):
-                    send(lam_out.at[other], lam_in.at[mine], lam_sem.at[0], lam_sem.at[1], peer)
-                lam_in[mine] = lam_out[mine]
+                give_back(lam_out, lam_in, lam_sem)
                 break
             lam = lam_next
             if step == 0:
@@ -797,9 +826,7 @@
             if step == ITERS - 2:
                 for i in range(plane):
                     x_out[i] = changes[i]
-                for other, peer in zip(others, mates):
-                    send(x_out.at[other], x_in.at[mine], x_sem.at[0], x_sem.at[1], peer)
-                x_in[mine] = x_out[mine]
+                give_back(x_out, x_in, x_sem)
         if step == 0:
             with jax.named_scope("P_relayr0"):
                 relay_half(0)
@@ -832,13 +859,21 @@
                 faces(step + 1, values[plane - 1][:, :width], values[0][:, width:])
 
     with jax.named_scope("P_uncorr1"):
-        uncorrected(early, tiles)
+        uncorrected(sooner, tiles)
     with jax.named_scope("P_qwait"):
         arrived(q_in.at[pl.ds(0, plane - 1)], q_sem.at[1])
-        q_ref[...] = q_in[...].reshape(q_ref.shape)
+    with jax.named_scope("P_last"):
+        high, low = split(q_in[...].reshape(columns, wide).T)
+        pair = jnp.concatenate([high, low], axis=1)
+        for c in range(tiles):
+            rows = pl.ds(c * tile, tile)
+            step = jnp.dot(kph_ref[rows, :], pair, preferred_element_type=F32)
+            step = step[:, :columns] + step[:, columns:]
+            u_ref[rows, :] = u_ref[rows, :] - (step + jnp.dot(kpl_ref[rows, :], high, preferred_element_type=F32))
+
     with jax.named_scope("P_lamwait"):
         arrived(lam_in.at[pl.ds(0, plane - 1)], lam_sem.at[1])
-        lam_ref[...] = lam_in[...].reshape(lam_ref.shape)
+        lam_ref[...] = lam_in[...].reshape(columns, width).T
     with jax.named_scope("P_sent"):
         others_part = pl.ds(0, plane - 1)
         sent(own_c.at[others_part], c_sem.at[0])
@@ -862,24 +897,10 @@
         sent(lam_out.at[others_part], lam_sem.at[0])
 
 
-def plane_finish(pre_ref, kph_ref, kpl_ref, q_ref, lam_ref, u_hbm, lam_hbm, u_ref, lam_out, sem):
-    tiles = sem.shape[0] - 1
-    tile = u_ref.shape[0] // tiles
-    columns = q_ref.shape[0]
-    lam_out[...] = lam_ref[...].T
-    copies = [pltpu.make_async_copy(lam_out, lam_hbm, sem.at[tiles])]
-    copies[0].start()
-    high, low = split(q_ref[...])
-    pair = jnp.concatenate([high, low], axis=0)
-    for c in range(tiles):
-        rows = pl.ds(c * tile, tile)
-        both = lax.dot_general(kph_ref[rows, :], pair, NT, preferred_element_type=F32)
-        both = both[:, :columns] + both[:, columns:]
-        u_ref[rows, :] = pre_ref[rows, :] - (
-            both + lax.dot_general(kpl_ref[rows, :], high, NT, preferred_element_type=F32)
-        )
-        copies.append(pltpu.make_async_copy(u_ref.at[rows, :], u_hbm.at[rows, :], sem.at[c]))
-        copies[-1].start()
+def plane_finish(u_ref, lam_ref, u_hbm, lam_hbm, sem):
+    copies = [pltpu.make_async_copy(u_ref, u_hbm, sem.at[0]), pltpu.make_async_copy(lam_ref, lam_hbm, sem.at[1])]
+    for copy in copies:
+        copy.start()
     for copy in copies:
         copy.wait()
 
@@ -901,6 +922,8 @@
         ((order, order), F32),
         ((order, order), BF16),
         ((order, order), BF16),
+        ((order, wide), BF16),
+        ((order, wide), BF16),
         ((order, both + wide), BF16),
         ((order, columns), BF16),
         ((order, columns), BF16),
@@ -943,7 +966,6 @@
     outer, inner = grid_of(count)
     tile = 256 if order % 256 == 0 else order
     tiles = order // tile
-    pieces = tiles // 2 if tiles % 2 == 0 else 1
     plane, buffers = plane_scratch(count, order, columns, owned, total, width, primal)
     needed = size_of(buffers)
     wide = lanes_of(primal)
@@ -958,13 +980,10 @@
         functools.partial(plane_kernel, count, primal, width),
         out_shape=(
             shape((order, columns), F32),
-            shape((order, wide), BF16),
-            shape((order, wide), BF16),
-            shape((columns, wide), F32),
-            shape((columns, width), F32),
+            shape((width, columns), F32),
         ),
         in_specs=[pl.BlockSpec(memory_space=pltpu.HBM)] * 6,
-        out_specs=(vmem,) * 5,
+        out_specs=(vmem,) * 2,
         scratch_shapes=[
             pltpu.SMEM(face_rows.shape, jnp.int32),
             pltpu.SMEM(primal_rows.shape, jnp.int32),
@@ -985,7 +1004,7 @@
             dma(()),
             dma((plane, 2)),
             dma((2,)),
-            dma((3, 2)),
+            dma((4, 2)),
             dma((4,)),
             dma((ITERS, 2)),
             dma((ITERS, 2)),
@@ -1000,10 +1019,10 @@
     return pl.pallas_call(
         plane_finish,
         out_shape=(shape((order, columns), F32), shape((width, columns), F32)),
-        in_specs=[vmem] * 5,
+        in_specs=[vmem] * 2,
         out_specs=(pl.BlockSpec(memory_space=pltpu.HBM),) * 2,
-        scratch_shapes=[pltpu.VMEM((order, columns), F32), pltpu.VMEM((width, columns), F32), dma((pieces + 1,))],
-        compiler_params=pltpu.CompilerParams(vmem_limit_bytes=4 * order * columns * 8),
+        scratch_shapes=[dma((2,))],
+        compiler_params=pltpu.CompilerParams(vmem_limit_bytes=4 * order * columns * 4),
     )(*parts)
 
 

time: 38.8 us -> 38.3 us (0.987)
  Pallas kernels: 38 us -> 37.5 us
where the time goes in v3:
time: 38.3 us; the launch traced here: 38.1 us
  Pallas kernels  37.5 us (98%)
  between operations  0.64 us (2%)
    pallas_call x1, Pallas kernels, planar(): pl.pallas_call(functools.partial(plane_kernel, count, primal, width), out...  36.6 us
    pallas_call x1, Pallas kernels, planar(): pl.pallas_call(plane_finish, out_shape=(shape((order, columns), F32), sha...  0.91 us

profile of v3, /device:TPU:0, one launch (start us, length us, event | category | flops | bytes accessed | tf_op | source)
XLA Modules:
  0.0 38.1 jit_solution(3581338218118927457)
XLA Ops:
  0.6 36.6 %shard_map.77 = (f32[1536,128]{1,0:T(8,128)S(1)}, f32[128,128]{1,0:T(8,128)S(1)}) custom-call(s32[1,2,128]{2,1,0:T(2,128)} %face_hbm.1, s32[1,96]{1,0:T(1,128)} %prim_hbm.1, s32[1,96]{1,0:T(1,128)} %slot_hbm.1, f32[1536,1536]{1,0:T(8,128)} %k_hbm.1, f32[1536,128]{1,0:T(8,128)} %f_hbm.1, f32[48,768]{1,0:T(8,128)} %cinv_hbm.1), custom_call_target="tpu_custom_call" | custom-call | tf_op jit(solution)/shard_map/pallas_call | solution.py:979
  37.2 0.9 %shard_map.78 = (f32[1536,128]{1,0:T(8,128)}, f32[128,128]{1,0:T(8,128)}) custom-call(f32[1536,128]{1,0:T(8,128)S(1)} %get-tuple-element.4.u_ref, f32[128,128]{1,0:T(8,128)S(1)} %get-tuple-element.5.lam_ref), custom_call_target="tpu_custom_call" | custom-call | tf_op jit(solution)/shard_map/pallas_call | solution.py:1019

commit v4 on v3

--- a/solution.py
+++ b/solution.py
@@ -607,25 +607,41 @@
     def face_part(ref, step):
         return ref.at[step] if step + 1 < ITERS else ref.at[step, pl.ds(0, 1)]
 
-    urgent = jnp.where(mine == 0, 1, 0)
+    rim = (mine == 0) | (mine == plane - 1)
+
+    def urgent_half(block):
+        return jnp.where(block == 0, 1, 0)
 
     def spread_half(half):
         for peer in across_peers + [partner]:
             rows = ar_ref.at[mine, half]
             send(rows, rows, ar_send, ar_recv.at[mine, half], peer)
 
-    def relay_half(flip):
-        for other in across:
-            half = jnp.where(other == 0, 1 - flip, flip)
-            rows = ar_ref.at[other, half]
-            arrived(rows, ar_recv.at[other, half])
-            send(rows, rows, ar_send, ar_recv.at[other, half], partner)
-
-    def settle_half(flip):
-        for other in [mine] + across:
-            block = other + 1 - 2 * core
-            half = jnp.where(block == 0, 1 - flip, flip)
-            arrived(ar_ref.at[block, half], ar_recv.at[block, half])
+    def relay_half(block, half):
+        rows = ar_ref.at[block, half]
+        arrived(rows, ar_recv.at[block, half])
+        send(rows, rows, ar_send, ar_recv.at[block, half], partner)
+
+    def spread_rows():
+        half = urgent_half(mine)
+        spread_half(half)
+        spread_half(1 - half)
+
+    def relay_urgent():
+        relay_half(across[0], urgent_half(across[0]))
+
+    def relay_whole():
+        relay_half(across[0], 0)
+        relay_half(across[0], 1)
+
+    def relay_second():
+        relay_half(across[0], 1 - urgent_half(across[0]))
+
+    first_block = jnp.where(core == 0, plane - 1, 0)
+    second_block = mine + across[0] + 2 - 4 * core - first_block
+
+    def settle_half(block, half):
+        arrived(ar_ref.at[block, half], ar_recv.at[block, half])
 
     with jax.named_scope("P_first"):
         picked(both, primal, lambda i: prim_s[0, i])
@@ -661,8 +677,7 @@
         found = columns_of(slice(0, both), e_ref[:, :both])
         ar_ref[mine, 0] = found[:width]
         ar_ref[mine, 1] = found[width:]
-        spread_half(urgent)
-        spread_half(1 - urgent)
+        pl.when(rim)(spread_rows)
     with jax.named_scope("P_relayac"):
         relay(ac_ref, ac_send, ac_recv)
     pl.when(mine == 1)(last_edge)
@@ -672,6 +687,7 @@
     faces(0, b_in[plane - 1, :, :width], b_in[0, :, width:])
     with jax.named_scope("P_halve"):
         halve(0, tiles)
+    pl.when(jnp.logical_not(rim))(spread_rows)
 
     def primal_columns(first_tile, last_tile):
         picks = e_ref[:, both:]
@@ -695,7 +711,7 @@
                 ref[i, primal:, :] = jnp.zeros((wide - primal, both), BF16)
 
     early = tiles // 3
-    sooner = jnp.where(mine < 2, early // 2, early)
+    sooner = jnp.where(mine == 1, early // 2, early)
     with jax.named_scope("P_halo"):
         settle_coarse()
         near = cinv_ref.at[0]
@@ -820,17 +836,17 @@
                     settle(ap_ref, ap_recv)
                     halves_of((aph_ref, apl_ref), ap_ref)
             changes = [jnp.concatenate([-lam[i + 1], lam[i]], axis=1) for i in range(plane)]
-            publish(step + 1, [
-                c_in[i] + tall(changes[i], aph_ref[i], apl_ref[i], NT) for i in range(plane)
-            ])
             if step == ITERS - 2:
                 for i in range(plane):
                     x_out[i] = changes[i]
                 give_back(x_out, x_in, x_sem)
+            publish(step + 1, [
+                c_in[i] + tall(changes[i], aph_ref[i], apl_ref[i], NT) for i in range(plane)
+            ])
         if step == 0:
             with jax.named_scope("P_relayr0"):
-                relay_half(0)
-                settle_half(0)
+                pl.when(jnp.logical_not(rim))(relay_urgent)
+                settle_half(first_block, urgent_half(first_block))
                 for i, half in ((plane - 1, 0), (0, 1)):
                     rows = slice(half * width, (half + 1) * width)
                     for ref, part in zip((arh_ref, arl_ref), split(ar_ref[i, half])):
@@ -842,11 +858,14 @@
             with jax.named_scope("P_primcol0"):
                 primal_columns(0, early)
             with jax.named_scope("P_relayr1"):
-                relay_half(1)
+                pl.when(rim)(relay_whole)
+                pl.when(jnp.logical_not(rim))(relay_second)
             with jax.named_scope("P_primcol0"):
                 primal_columns(early, tiles - early)
             with jax.named_scope("P_settler1"):
-                settle_half(1)
+                settle_half(first_block, 1 - urgent_half(first_block))
+                settle_half(second_block, 0)
+                settle_half(second_block, 1)
                 for i in range(plane):
                     for half in range(2):
                         if (i, half) not in ((plane - 1, 0), (0, 1)):

time: 38.3 us -> 38.3 us (level)
  no operation moved by 1% of the time
where the time goes in v4:
time: 38.3 us; the launch traced here: 38.1 us
  Pallas kernels  37.5 us (98%)
  between operations  0.64 us (2%)
    pallas_call x1, Pallas kernels, planar(): pl.pallas_call(functools.partial(plane_kernel, count, primal, width), out...  36.6 us
    pallas_call x1, Pallas kernels, planar(): pl.pallas_call(plane_finish, out_shape=(shape((order, columns), F32), sha...  0.91 us

profile of v4, /device:TPU:0, one launch (start us, length us, event | category | flops | bytes accessed | tf_op | source)
XLA Modules:
  0.0 38.1 jit_solution(7498994257212743004)
XLA Ops:
  0.6 36.6 %shard_map.77 = (f32[1536,128]{1,0:T(8,128)S(1)}, f32[128,128]{1,0:T(8,128)S(1)}) custom-call(s32[1,2,128]{2,1,0:T(2,128)} %face_hbm.1, s32[1,96]{1,0:T(1,128)} %prim_hbm.1, s32[1,96]{1,0:T(1,128)} %slot_hbm.1, f32[1536,1536]{1,0:T(8,128)} %k_hbm.1, f32[1536,128]{1,0:T(8,128)} %f_hbm.1, f32[48,768]{1,0:T(8,128)} %cinv_hbm.1), custom_call_target="tpu_custom_call" | custom-call | tf_op jit(solution)/shard_map/pallas_call | solution.py:998
  37.2 0.9 %shard_map.78 = (f32[1536,128]{1,0:T(8,128)}, f32[128,128]{1,0:T(8,128)}) custom-call(f32[1536,128]{1,0:T(8,128)S(1)} %get-tuple-element.4.u_ref, f32[128,128]{1,0:T(8,128)S(1)} %get-tuple-element.5.lam_ref), custom_call_target="tpu_custom_call" | custom-call | tf_op jit(solution)/shard_map/pallas_call | solution.py:1038

commit v5 on v4

--- a/solution.py
+++ b/solution.py
@@ -373,8 +373,8 @@
     order, columns = f_ref.shape
     owned = primal // 2
     total = cinv_ref.shape[-1]
-    tiles = k_sem.shape[0]
-    tile = order // tiles
+    tile = 256 if order % 256 == 0 else order
+    tiles = order // tile
     share = columns // plane
     both = 2 * width
     wide = lanes_of(primal)
@@ -425,6 +425,11 @@
     def sent(ref, ssem):
         remote(ref, ref, ssem, r_sem.at[0, 1], partner).wait_send()
 
+    barrier = pltpu.get_barrier_semaphore()
+    greeted = mates + beyond + ([after, before] if outer % 2 == 0 else [])
+    for peer in greeted:
+        pl.semaphore_signal(barrier, inc=1, device_id={"sub": peer}, device_id_type=MESH)
+
     ints = [
         pltpu.make_async_copy(src, dst, in_sem.at[i])
         for i, (src, dst) in enumerate((
@@ -436,17 +441,12 @@
 
     def k_copy(c):
         rows = pl.ds(c * tile, tile)
-        return pltpu.make_async_copy(k_hbm.at[rows, :], k_ref.at[rows, :], k_sem.at[c])
+        return pltpu.make_async_copy(k_hbm.at[rows, :], k_ref.at[rows, :], k_sem)
 
     for copy in ints + [cinv_copy, f_copy]:
         copy.start()
     for c in range(tiles):
         k_copy(c).start()
-
-    barrier = pltpu.get_barrier_semaphore()
-    greeted = mates + beyond + ([after, before] if outer % 2 == 0 else [])
-    for peer in greeted:
-        pl.semaphore_signal(barrier, inc=1, device_id={"sub": peer}, device_id_type=MESH)
 
     with jax.named_scope("P_ints"):
         for copy in ints:
@@ -552,8 +552,7 @@
             kl_ref[rows, :] = low
 
     with jax.named_scope("P_kwait"):
-        for c in range(tiles):
-            k_copy(c).wait()
+        pltpu.make_async_copy(k_hbm, k_ref, k_sem).wait()
 
     def picked(start, size, row_at):
         @pl.loop(0, size // 8)
@@ -1011,7 +1010,7 @@
             pltpu.VMEM(primal_slot.shape, jnp.int32),
         ] + [pltpu.VMEM(size, kind) for size, kind in buffers] + [
             dma((7,)),
-            dma((tiles,)),
+            dma(()),
             dma((2,)),
             dma((2,)),
             dma(()),

time: 38.3 us -> 38.4 us (level)
  no operation moved by 1% of the time
where the time goes in v5:
time: 38.4 us; the launch traced here: 38.2 us
  Pallas kernels  37.6 us (98%)
  between operations  0.64 us (2%)
    pallas_call x1, Pallas kernels, planar(): pl.pallas_call(functools.partial(plane_kernel, count, primal, width), out...  36.7 us
    pallas_call x1, Pallas kernels, planar(): pl.pallas_call(plane_finish, out_shape=(shape((order, columns), F32), sha...  0.91 us

profile of v5, /device:TPU:0, one launch (start us, length us, event | category | flops | bytes accessed | tf_op | source)
XLA Modules:
  0.0 38.2 jit_solution(8175395749000434155)
XLA Ops:
  0.6 36.7 %shard_map.77 = (f32[1536,128]{1,0:T(8,128)S(1)}, f32[128,128]{1,0:T(8,128)S(1)}) custom-call(s32[1,2,128]{2,1,0:T(2,128)} %face_hbm.1, s32[1,96]{1,0:T(1,128)} %prim_hbm.1, s32[1,96]{1,0:T(1,128)} %slot_hbm.1, f32[1536,1536]{1,0:T(8,128)} %k_hbm.1, f32[1536,128]{1,0:T(8,128)} %f_hbm.1, f32[48,768]{1,0:T(8,128)} %cinv_hbm.1), custom_call_target="tpu_custom_call" | custom-call | tf_op jit(solution)/shard_map/pallas_call | solution.py:997
  37.3 0.9 %shard_map.78 = (f32[1536,128]{1,0:T(8,128)}, f32[128,128]{1,0:T(8,128)}) custom-call(f32[1536,128]{1,0:T(8,128)S(1)} %get-tuple-element.4.u_ref, f32[128,128]{1,0:T(8,128)S(1)} %get-tuple-element.5.lam_ref), custom_call_target="tpu_custom_call" | custom-call | tf_op jit(solution)/shard_map/pallas_call | solution.py:1037
